TPU v7x, 768 devices: a whole 4x8x12 slice. The times are simulated.
768 devices in a mesh: lat: 24 (over z, core), lon: 32 (over y, x).
Axes of the slice: x: 4, y: 8, z: 12, core: 2. Of those that a mesh axis runs over, the one named last changes fastest.
Arguments:
- queries: bfloat16 [48, 2048, 2048], P('lat', 'lon'), may hold values from -50 to 50
- keyval: bfloat16 [2, 48, 2048, 2048], P(None, 'lat', 'lon'), may hold values from -5 to 5
- keep: int32 [48], replicated, may hold values from 0 to 1, as said below
- lists: int32 [48, 64, 13], P('lat', 'lon'), may hold values from 0 to 14, as said below
Outputs:
- attended: bfloat16 [48, 2048, 2048], P('lat', 'lon')
- gram_factor: float32 [24, 16, 128, 128], P('lat')
Inputs may be any that keep to these rules, and one draw needn't show every extreme that they name: `lists`: each list holds 13 different candidate numbers; its first is 7, the query block itself. keep is 0 in rows 0 and 47, and 1 outside the first and last 12 rows.
All inputs are finite; a program needn't handle non-finite values.
Results may differ from a plain program's by a relative error of at most 0.015.
Values may be sent and summed in bfloat16 or wider, within the bound.
No kernel may reach another device: no remote copies, remote signals or barrier semaphores. Data moves between devices by JAX's collectives and lax.ppermute only.
A program may use at most 64 MiB of HBM per device.

v0:
```python
import jax
import jax.numpy as jnp
from jax import lax
from jax.sharding import PartitionSpec as P

HEADS = 16
HD = 128
BLOCK = 32
HALO = 2
CAND = 15


def extended(x, sides, width):
    for axis, dim in sides:
        size, length = (lax.axis_size(axis), x.shape[dim])
        up = [(i, (i + 1) % size) for i in range(size - 1)]
        down = [(j, i) for i, j in up]
        last = lax.slice_in_dim(x, length - width, length, axis=dim)
        leading = lax.slice_in_dim(x, 0, width, axis=dim)
        before = lax.ppermute(last, axis, up)
        after = lax.ppermute(leading, axis, down)
        x = jnp.concatenate([before, x, after], axis=dim)
    return x


def from_behind(x, axis, by):
    length = lax.axis_size(axis)
    return lax.ppermute(x, axis, [(i, (i + by) % length) for i in range(length)])


def visible_blocks(keep, lists, tile_rows):
    first_row = lax.axis_index("lat") * tile_rows
    total_rows = tile_rows * lax.axis_size("lat")
    padded = jnp.pad(keep, (HALO, HALO))
    local_keep = lax.dynamic_slice_in_dim(padded, first_row, tile_rows + 2 * HALO)
    ext_rows = (
        jnp.arange(tile_rows, dtype=jnp.int32)[:, None]
        + jnp.arange(2 * HALO + 1, dtype=jnp.int32)[None, :]
    )
    global_row = first_row + ext_rows - HALO
    inside = (global_row >= 0) & (global_row < total_rows)
    centre = (jnp.arange(2 * HALO + 1) == HALO)[None, :]
    row_ok = inside & (centre | (local_keep[ext_rows] == 1))
    listed = jnp.any(lists[..., None] == jnp.arange(CAND, dtype=jnp.int32), axis=2)
    return listed & jnp.repeat(row_ok, 3, axis=1)[:, None, :]


def local(queries, keyval, keep, lists):
    tile_rows, tile_cols, features = queries.shape
    blocks = tile_cols // BLOCK
    tall_band = extended(keyval, (("lat", 1),), HALO)
    west_keys = from_behind(tall_band[:, :, tile_cols - BLOCK :], "lon", 1)
    east_keys = from_behind(tall_band[:, :, :BLOCK], "lon", -1)
    wide_band = jnp.concatenate([west_keys, tall_band, east_keys], axis=2)
    wide_band = wide_band.reshape(2, tile_rows + 2 * HALO, blocks + 2, BLOCK, HEADS, HD)
    qblocks = queries.reshape(tile_rows, blocks, BLOCK, HEADS, HD)
    allowed = visible_blocks(keep, lists, tile_rows)
    gathered = []
    for offset in range(2 * HALO + 1):
        for lon_step in range(3):
            gathered.append(wide_band[:, offset : offset + tile_rows, lon_step : lon_step + blocks])
    cand_band = jnp.concatenate(gathered, axis=3)
    scores = jnp.einsum(
        "tbqhe,tbkhe->tbhqk", qblocks, cand_band[0], preferred_element_type=jnp.float32
    ) * HD ** (-0.5)
    key_mask = jnp.repeat(allowed, BLOCK, axis=2)[:, :, None, None, :]
    scores = jnp.where(key_mask, scores, -jnp.inf)
    row_top = jnp.max(scores, axis=-1, keepdims=True)
    weights = jnp.exp(scores - row_top)
    denominator = jnp.sum(weights, axis=-1)
    rounded = weights.astype(jnp.bfloat16)
    mixture = jnp.einsum(
        "tbhqk,tbkhe->tbqhe", rounded, cand_band[1], preferred_element_type=jnp.float32
    )
    attended = (mixture / jnp.transpose(denominator, (0, 1, 3, 2))[..., None]).astype(jnp.bfloat16)
    flat_rows = attended.reshape(tile_rows * tile_cols, HEADS, HD)
    partial_value = jnp.einsum(
        "nhd,nhe->hde", flat_rows, flat_rows, preferred_element_type=jnp.float32
    )
    gram_sum = lax.psum(partial_value.astype(jnp.bfloat16), "lon").astype(jnp.float32)
    return (attended.reshape(tile_rows, tile_cols, features), gram_sum[None])


def solution(mesh):
    placed = (P("lat", "lon", None), P(None, "lat", "lon", None), P(), P("lat", "lon", None))
    return jax.shard_map(
        local,
        mesh=mesh,
        in_specs=placed,
        out_specs=(P("lat", "lon", None), P("lat", None, None, None)),
        check_vma=False,
    )
```

profile of v0, /device:TPU:64, one launch (start us, length us, event | category | flops | bytes accessed | tf_op | source)
XLA Modules:
  0.0 292.8 jit_solution(4298495876355573468)
XLA Ops:
  7.2 1.9 collective-permute-start
  9.2 3.6 %collective-permute-start.1 = (bf16[2,2,64,2048]{3,2,1,0:T(8,128)(2,1)}, bf16[2,2,64,2048]{3,2,1,0:T(8,128)(2,1)S(1)}, u32[]{:S(2)}, u32[]{:S(2)}) collective-permute-start(bf16[2,2,64,2048]{3,2,1,0:T(8,128)(2,1)} %param.5), channel_id=1, source_target_pairs={{32,0},{64,32},{96,64},{128,96},{160,128},{192,160},{224,192},{256... | collective-permute-start | bytes 3145736 | tf_op jit(solution)/shard_map/ppermute | solution.py:21
  12.8 10.7 %collective-permute-done = bf16[2,2,64,2048]{3,2,1,0:T(8,128)(2,1)S(1)} collective-permute-done((bf16[2,2,64,2048]{3,2,1,0:T(8,128)(2,1)}, bf16[2,2,64,2048]{3,2,1,0:T(8,128)(2,1)S(1)}, u32[]{:S(2)}, u32[]{:S(2)}) %collective-permute-start) | collective-permute-done | bytes 1048608 | tf_op jit(solution)/shard_map/ppermute | solution.py:20
  23.6 0.1 constant_dynamic-update-slice_fusion.2
  23.7 1.3 constant_dynamic-update-slice_fusion.1
  25.0 0.5 collective-permute-done.1
  25.4 0.1 constant_dynamic-update-slice_fusion
  25.5 1.9 fusion.26
  27.4 3.4 %collective-permute-start.2 = (bf16[2,6,32,2048]{3,2,1,0:T(8,128)(2,1)}, bf16[2,6,32,2048]{3,2,1,0:T(8,128)(2,1)}, u32[]{:S(2)}, u32[]{:S(2)}) collective-permute-start(bf16[2,6,32,2048]{3,2,1,0:T(8,128)(2,1)} %get-tuple-element.17), channel_id=1, source_target_pairs={{0,1},{1,2},{2,3},{3,4},{4,5},{5,6},{6,7},{7,8},{8,9},{9,10},{10,1... | collective-permute-start | bytes 4718600 | tf_op jit(solution)/shard_map/ppermute | solution.py:28
  30.8 6.1 %collective-permute-start.3 = (bf16[2,6,32,2048]{3,2,1,0:T(8,128)(2,1)}, bf16[2,6,32,2048]{3,2,1,0:T(8,128)(2,1)}, u32[]{:S(2)}, u32[]{:S(2)}) collective-permute-start(bf16[2,6,32,2048]{3,2,1,0:T(8,128)(2,1)} %get-tuple-element.18), channel_id=1, source_target_pairs={{0,31},{1,0},{2,1},{3,2},{4,3},{5,4},{6,5},{7,6},{8,7},{9,8},{10,9... | collective-permute-start | bytes 4718600 | tf_op jit(solution)/shard_map/ppermute | solution.py:28
  36.9 0.1 reshape.56
  37.0 0.1 pad_dynamic-slice_fusion
  37.1 0.7 gather_fusion
  37.8 0.1 reshape.64
  37.9 0.1 and.18
  38.0 0.1 fusion.22
  38.2 0.1 broadcast_in_dim.35
  38.2 0.1 broadcast_in_dim.36
  38.3 2.0 copy.64
  40.3 28.3 %collective-permute-done.2 = bf16[2,6,32,2048]{3,2,1,0:T(8,128)(2,1)} collective-permute-done((bf16[2,6,32,2048]{3,2,1,0:T(8,128)(2,1)}, bf16[2,6,32,2048]{3,2,1,0:T(8,128)(2,1)}, u32[]{:S(2)}, u32[]{:S(2)}) %collective-permute-start.2) | collective-permute-done | bytes 1572896 | tf_op jit(solution)/shard_map/ppermute | solution.py:28
  68.6 1.7 collective-permute-done.3
  70.3 2.8 pad_maximum_fusion
  73.1 2.3 copy.63
  75.5 6.2 %fusion.25 = (bf16[2,2,2,32,16,128]{5,4,3,2,1,0:T(8,128)(2,1)S(1)}, bf16[2,2,2,32,16,128]{5,4,3,2,1,0:T(8,128)(2,1)S(1)}, bf16[2,2,2,32,16,128]{5,4,3,2,1,0:T(8,...) fusion(bf16[2,6,4,32,16,128]{5,4,3,2,1,0:T(8,128)(2,1)S(1)} %bi, ...), kind=kLoop, calls=%fused_computation.52 | loop fusion | bytes 31457280 | tf_op jit(solution)/shard_map/slice | solution.py:61
  81.7 0.3 copy_dynamic-update-slice_fusion.14
  82.0 0.3 copy_dynamic-update-slice_fusion.13
  82.3 0.3 copy_dynamic-update-slice_fusion.12
  82.7 0.3 copy_dynamic-update-slice_fusion.11
  83.0 0.3 copy_dynamic-update-slice_fusion.10
  83.4 0.3 copy_dynamic-update-slice_fusion.9
  83.7 0.3 copy_dynamic-update-slice_fusion.8
  84.1 0.3 copy_dynamic-update-slice_fusion.7
  84.4 0.3 copy_dynamic-update-slice_fusion.6
  84.8 0.3 copy_dynamic-update-slice_fusion.5
  85.1 0.3 copy_dynamic-update-slice_fusion.4
  85.5 0.3 copy_dynamic-update-slice_fusion.3
  85.8 0.3 copy_dynamic-update-slice_fusion.2
  86.2 0.3 copy_dynamic-update-slice_fusion.1
  86.5 0.3 copy_dynamic-update-slice_fusion
  86.9 5.5 %copy-done.1 = bf16[2,2,2,480,16,128]{5,3,4,2,1,0:T(8,128)(2,1)} copy-done((bf16[2,2,2,480,16,128]{5,3,4,2,1,0:T(8,128)(2,1)}, bf16[2,2,2,480,16,128]{5,3,4,2,1,0:T(8,128)(2,1)S(1)}, u32[]{:S(2)}) %copy-start.1) | copy-done | bytes 15728664
  92.4 6.4 %bitcast_reduce_fusion = (f32[2,2,16,32]{3,2,1,0:T(8,128)S(1)}, f32[2,2,16,480,32]{3,4,2,1,0:T(8,128)S(1)}) fusion(pred[2,2,480]{2,1,0:T(4,128)(4,1)S(1)} %broadcast_in_dim.36, bf16[2,2,32,16,128]{4,3,2,1,0:T(8,128)(2,1)S(1)} %bitcast.57, bf16[2,2,2,480,16,128]{5,3,4,2,1,0:T(8,128)(2,1)} %copy-done.1), kind=kOutput, calls=%fused_computation.7 | convolution fusion | flops 254605312 | bytes 12330880 | tf_op jit(solution)/shard_map/tbqhe,tbkhe->tbhqk/dot_general | solution.py:63
  98.8 1.3 fusion.3
  100.1 5.3 %fusion.17 = bf16[2,2,32,16,128]{4,2,3,1,0:T(8,128)(2,1)S(1)} fusion(bf16[2,2,2,480,16,128]{5,3,4,2,1,0:T(8,128)(2,1)} %copy-done.1, f32[2,2,16,480,32]{3,4,2,1,0:T(8,128)S(1)} %get-tuple-element.20, f32[2,2,16,32]{3,2,1,0:T(8,128)S(1)} %get-tuple-element.19, pred[2,2,480]{2,1,0:T(4,128)(4,1)S(1)} %broadcast_in_dim.36, f32[2,2,32,16]{2,3,1,0:T(8,128)S(1)} %bitcast.58), kind=kOutput, calls=%fused_computation.20 | convolution fusion | flops 256114688 | bytes 12339072 | tf_op jit(solution)/shard_map/tbhqk,tbkhe->tbqhe/dot_general | solution.py:72
  105.5 0.2 copy.44
  105.7 1.1 fusion.13
  106.8 1.0 reshape.52
  107.9 176.0 %all-reduce.3.cloned.1.call-done = bf16[1,16,128,128]{3,2,1,0:T(8,128)(2,1)} async-done(((bf16[1,16,128,128]{3,2,1,0:T(8,128)(2,1)}), bf16[1,16,128,128]{3,2,1,0:T(8,128)(2,1)}) %all-reduce.3.cloned.1.call-update) | async-done | bytes 524304 | tf_op jit(solution)/shard_map/psum | solution.py:80
  283.8 2.1 broadcast_in_dim.40
  (16 shorter events, 0.2 us)
Async XLA Ops:
  7.2 29.8 %copy-start.3 = (s32[48]{0:T(128)S(1)}, s32[48]{0:T(128)}, u32[]{:S(2)}) copy-start(s32[48]{0:T(128)} %param.6) | copy-start | bytes 580
  7.2 30.9 %copy-start.2 = (s32[2,2,13]{2,1,0:T(2,128)S(1)}, s32[2,2,13]{2,1,0:T(2,128)}, u32[]{:S(2)}) copy-start(s32[2,2,13]{2,1,0:T(2,128)} %param.7) | copy-start | bytes 628
  7.2 276.6 %all-reduce.3.cloned.1.call-start = ((), (), s32[]{:S(2)}) async-start(), calls=%async_computation | async-start | bytes 1048576 | tf_op jit(solution)/shard_map/psum | solution.py:80
  7.2 16.3 %collective-permute-start = (bf16[2,2,64,2048]{3,2,1,0:T(8,128)(2,1)}, bf16[2,2,64,2048]{3,2,1,0:T(8,128)(2,1)S(1)}, u32[]{:S(2)}, u32[]{:S(2)}) collective-permute-start(bf16[2,2,64,2048]{3,2,1,0:T(8,128)(2,1)} %param.5), channel_id=1, source_target_pairs={{0,32},{32,64},{64,96},{96,128},{128,160},{160,192},{192,224},{224... | collective-permute-start | bytes 3145736 | tf_op jit(solution)/shard_map/ppermute | solution.py:20
  9.2 16.3 %collective-permute-start.1 = (bf16[2,2,64,2048]{3,2,1,0:T(8,128)(2,1)}, bf16[2,2,64,2048]{3,2,1,0:T(8,128)(2,1)S(1)}, u32[]{:S(2)}, u32[]{:S(2)}) collective-permute-start(bf16[2,2,64,2048]{3,2,1,0:T(8,128)(2,1)} %param.5), channel_id=1, source_target_pairs={{32,0},{64,32},{96,64},{128,96},{160,128},{192,160},{224,192},{256... | collective-permute-start | bytes 3145736 | tf_op jit(solution)/shard_map/ppermute | solution.py:21
  27.4 41.2 %collective-permute-start.2 = (bf16[2,6,32,2048]{3,2,1,0:T(8,128)(2,1)}, bf16[2,6,32,2048]{3,2,1,0:T(8,128)(2,1)}, u32[]{:S(2)}, u32[]{:S(2)}) collective-permute-start(bf16[2,6,32,2048]{3,2,1,0:T(8,128)(2,1)} %get-tuple-element.17), channel_id=1, source_target_pairs={{0,1},{1,2},{2,3},{3,4},{4,5},{5,6},{6,7},{7,8},{8,9},{9,10},{10,1... | collective-permute-start | bytes 4718600 | tf_op jit(solution)/shard_map/ppermute | solution.py:28
  30.8 39.5 %collective-permute-start.3 = (bf16[2,6,32,2048]{3,2,1,0:T(8,128)(2,1)}, bf16[2,6,32,2048]{3,2,1,0:T(8,128)(2,1)}, u32[]{:S(2)}, u32[]{:S(2)}) collective-permute-start(bf16[2,6,32,2048]{3,2,1,0:T(8,128)(2,1)} %get-tuple-element.18), channel_id=1, source_target_pairs={{0,31},{1,0},{2,1},{3,2},{4,3},{5,4},{6,5},{7,6},{8,7},{9,8},{10,9... | collective-permute-start | bytes 4718600 | tf_op jit(solution)/shard_map/ppermute | solution.py:28
  84.4 8.0 %copy-start = (bf16[16,8,16,128]{3,2,1,0:T(8,128)(2,1)S(1)}, bf16[16,8,16,128]{3,2,1,0:T(8,128)(2,1)}, u32[]{:S(2)}) copy-start(bf16[16,8,16,128]{3,2,1,0:T(8,128)(2,1)} %copy.64) | copy-start | bytes 1572868
  86.8 5.5 %copy-start.1 = (bf16[2,2,2,480,16,128]{5,3,4,2,1,0:T(8,128)(2,1)}, bf16[2,2,2,480,16,128]{5,3,4,2,1,0:T(8,128)(2,1)S(1)}, u32[]{:S(2)}) copy-start(bf16[2,2,2,480,16,128]{5,3,4,2,1,0:T(8,128)(2,1)S(1)} %copy_dynamic-update-slice_fusion) | copy-start | bytes 47185924
Sparse Core Ops, SparseCore 0:
  107.0 176.8 all-reduce.2
where the time goes:
time: 293 us
  waiting for transfers between devices  217 us (74%)
  local copies, waits for them, and re-layouts  26.9 us (9%)
  starting transfers between devices  15.1 us (5%)
  between operations  14.3 us (5%)
  matrix products  12.9 us (4%)
  other arithmetic  6.37 us (2%)
    psum x1, waiting for transfers between devices, local(): lax.psum(partial_value.astype(jnp.bfloat16), 'lon').astype(jnp.float32)  176 us
    ppermute x2, waiting for transfers between devices, from_behind(): lax.ppermute(x, axis, [(i, (i + by) % length) for i in range(length)])  30.1 us
    unnamed x26, local copies, waits for them, and re-layouts  15.9 us
    ppermute x1, waiting for transfers between devices, extended(): before = lax.ppermute(last, axis, up)  10.7 us
    ppermute x2, starting transfers between devices, from_behind(): lax.ppermute(x, axis, [(i, (i + by) % length) for i in range(length)])  9.48 us
    dot_general x1, matrix products, local(): jnp.einsum('tbqhe,tbkhe->tbhqk', qblocks, cand_band[0], preferred_element...  6.44 us
    slice x1, local copies, waits for them, and re-layouts, local(): wide_band[:, offset:offset + tile_rows, lon_step:lon_step + blocks]  6.23 us
  transfers between devices with their start and end apart: 5, of which 5 were waited for; matrix products, arithmetic and copies ran while one was open for 2% of the time, Pallas kernels for 0%

commit v1 on v0

v1 whole, which is shorter than its diff:
```python
import functools

import jax
import jax.numpy as jnp
from jax import lax
from jax.experimental import pallas as pl
from jax.experimental.pallas import tpu as pltpu
from jax.sharding import PartitionSpec as P

HEADS = 16
HD = 128
BLOCK = 32
HALO = 2
CAND = 15
NB = 13
ROWS = 40
NEG = -1e30
LOG2 = 1.4426950408889634 * HD ** (-0.5)

VMEM = pl.BlockSpec(memory_space=pltpu.VMEM)
SMEM = pl.BlockSpec(memory_space=pltpu.SMEM)


def iota(shape, axis):
    return lax.broadcasted_iota(jnp.int32, shape, axis)


def prepare_body(rows_total, lat_ref, keep_ref, lists_ref, q_ref, west_ref, east_ref, own_ref):
    first = lat_ref[0] * 2
    lane = iota((1, 128), 1)
    for b, out in ((0, west_ref), (1, east_ref)):
        for t in range(2):
            listed = jnp.zeros((1, 128), jnp.int32)
            for n in range(NB):
                listed = jnp.where(lane == lists_ref[t, b, n], 1, listed)
            usable = jnp.zeros((1, 128), jnp.int32)
            for k in range(2 * HALO + 1):
                row = first + (t + k - HALO)
                inside = jnp.logical_and(row >= 0, row < rows_total)
                if k == HALO:
                    good = 1
                else:
                    good = jnp.where(inside, keep_ref[jnp.clip(row, 0, rows_total - 1)], 0)
                usable = jnp.where((lane >= 3 * k) & (lane < 3 * k + 3), good, usable)
            seen = jnp.where((listed == 1) & (usable == 1), 1.0, 0.0)
            seen = jnp.broadcast_to(seen, (BLOCK, 128)).astype(jnp.bfloat16)
            out[HEADS, t * BLOCK : (t + 1) * BLOCK, :] = seen
            own_ref[b, t * BLOCK : (t + 1) * BLOCK, :] = seen
            for h in range(HEADS):
                out[h, t * BLOCK : (t + 1) * BLOCK, :] = q_ref[
                    t, b * BLOCK : (b + 1) * BLOCK, h * HD : (h + 1) * HD
                ]


def bias_of(seen, t, b, key_blocks):
    width = len(key_blocks) * BLOCK
    cand = iota((128, 6 * width), 0)
    key = iota((128, 6 * width), 1)
    hit = jnp.zeros((128, 6 * width), jnp.bool_)
    for row in range(6):
        if 0 <= row - t <= 4:
            for n, kb in enumerate(key_blocks):
                if -1 <= kb - b <= 1:
                    c = 3 * (row - t) + (kb - b) + 1
                    low = row * width + n * BLOCK
                    hit = hit | ((cand == c) & (key >= low) & (key < low + BLOCK))
    spread = jnp.where(hit, 1.0, 0.0).astype(jnp.bfloat16)
    shown = jnp.dot(seen, spread, preferred_element_type=jnp.float32)
    return jnp.where(shown > 0.5, 0.0, NEG)


def rows_of(refs, part, blocks, h):
    cells = slice(blocks[0] * BLOCK, (blocks[-1] + 1) * BLOCK)
    return jnp.concatenate(
        [ref[part, r, cells, h * HD : (h + 1) * HD] for ref in refs for r in range(2)], axis=0
    )


def attend(q, keys, values, bias):
    scores = lax.dot_general(q, keys, (((1,), (1,)), ((), ())), preferred_element_type=jnp.float32)
    scores = scores * LOG2 + bias
    top = jnp.max(scores, axis=-1, keepdims=True)
    weights = jnp.exp2(scores - top)
    total = jnp.sum(weights, axis=-1, keepdims=True)
    mixed = jnp.dot(weights.astype(jnp.bfloat16), values, preferred_element_type=jnp.float32)
    return (mixed / total).astype(jnp.bfloat16), top + jnp.log2(total)


def remote_body(west_ref, east_ref, low_ref, own_ref, high_ref, to_west_ref, to_east_ref):
    refs = (low_ref, own_ref, high_ref)
    lane = iota((2 * BLOCK, 128), 1)
    for q_ref, out, b, kb, held in ((west_ref, to_west_ref, 1, 2, 0), (east_ref, to_east_ref, 0, -1, 1)):
        bias = jnp.concatenate(
            [bias_of(q_ref[HEADS, t * BLOCK : (t + 1) * BLOCK, :], t, b, (kb,)) for t in range(2)], axis=0
        )
        stats = jnp.zeros((2 * BLOCK, 128), jnp.float32)
        for h in range(HEADS):
            mixed, level = attend(
                q_ref[h], rows_of(refs, 0, (held,), h), rows_of(refs, 1, (held,), h), bias
            )
            out[h] = mixed
            stats = jnp.where(lane == h, level, stats)
        coarse = stats.astype(jnp.bfloat16).astype(jnp.float32)
        rest = stats - coarse
        middle = rest.astype(jnp.bfloat16).astype(jnp.float32)
        fine = rest - middle
        packed = coarse + pltpu.roll(middle, HEADS, 1) + pltpu.roll(fine, 2 * HEADS, 1)
        out[HEADS] = packed.astype(jnp.bfloat16)


def own_body(q_ref, seen_ref, low_ref, own_ref, high_ref, out_ref, level_ref):
    refs = (low_ref, own_ref, high_ref)
    lane = iota((4 * BLOCK, 128), 1)
    bias = jnp.concatenate(
        [
            bias_of(seen_ref[b, t * BLOCK : (t + 1) * BLOCK, :], t, b, (0, 1))
            for b in range(2)
            for t in range(2)
        ],
        axis=0,
    )
    stats = jnp.zeros((4 * BLOCK, 128), jnp.float32)
    for h in range(HEADS):
        q = jnp.concatenate(
            [
                q_ref[t, b * BLOCK : (b + 1) * BLOCK, h * HD : (h + 1) * HD]
                for b in range(2)
                for t in range(2)
            ],
            axis=0,
        )
        mixed, level = attend(q, rows_of(refs, 0, (0, 1), h), rows_of(refs, 1, (0, 1), h), bias)
        out_ref[h] = mixed
        stats = jnp.where(lane == h, level, stats)
    level_ref[...] = stats


def combine_body(own_ref, level_ref, west_ref, east_ref, out_ref, packed_ref):
    mine, theirs = [], []
    for b, ref in ((0, west_ref), (1, east_ref)):
        split = ref[HEADS].astype(jnp.float32)
        far = split + pltpu.roll(split, 128 - HEADS, 1) + pltpu.roll(split, 128 - 2 * HEADS, 1)
        near = level_ref[b * 2 * BLOCK : (b + 1) * 2 * BLOCK, :]
        top = jnp.maximum(near, far)
        near, far = jnp.exp2(near - top), jnp.exp2(far - top)
        both = near + far
        mine.append(near / both)
        theirs.append(far / both)
    row, lane = iota((64, 128), 0), iota((64, 128), 1)
    for h in range(HEADS):
        parts = []
        for b, ref in ((0, west_ref), (1, east_ref)):
            near = own_ref[h, b * 2 * BLOCK : (b + 1) * 2 * BLOCK, :].astype(jnp.float32)
            far = ref[h].astype(jnp.float32)
            part = (near * mine[b][:, h : h + 1] + far * theirs[b][:, h : h + 1]).astype(jnp.bfloat16)
            for t in range(2):
                out_ref[t, b * BLOCK : (b + 1) * BLOCK, h * HD : (h + 1) * HD] = part[
                    t * BLOCK : (t + 1) * BLOCK
                ]
            parts.append(part)
        cells = jnp.concatenate(parts, axis=0)
        gram = lax.dot_general(cells, cells, (((0,), (0,)), ((), ())), preferred_element_type=jnp.float32)
        upper, lower = gram[:64], gram[64:]
        folded = jnp.where((lane < 64) & (row > lane), pltpu.roll(lower, 64, 1), upper).astype(jnp.bfloat16)
        diagonal = jnp.sum(jnp.where(lane - 64 == row, lower, 0.0), axis=0, keepdims=True)
        diagonal = jnp.broadcast_to(diagonal, (8, 128)).astype(jnp.bfloat16)
        for half in range(2):
            packed_ref[2 * h + half, :32, :] = folded[half * 32 : (half + 1) * 32]
            packed_ref[2 * h + half, 32:, :] = diagonal


def sum_body(x_ref, out_ref):
    total = jnp.sum(x_ref[...].astype(jnp.float32), axis=0).astype(jnp.bfloat16)
    out_ref[...] = jnp.broadcast_to(total[None], out_ref.shape)


def unpack_body(x_ref, out_ref):
    row, lane = iota((64, 128), 0), iota((64, 128), 1)
    for h in range(HEADS):
        folded = jnp.concatenate([x_ref[2 * h, :32, :], x_ref[2 * h + 1, :32, :]], axis=0).astype(jnp.float32)
        diagonal = x_ref[2 * h, 32:, :].astype(jnp.float32)[:1]
        turned = jnp.concatenate([folded, jnp.zeros_like(folded)], axis=0).T
        out_ref[0, h, :64, :] = jnp.where((lane < 64) & (row > lane), turned[:64], folded)
        corner = pltpu.roll(jnp.where(row > lane, folded, turned[:64]), 64, 1)
        corner = jnp.where(lane - 64 == row, diagonal, corner)
        out_ref[0, h, 64:, :] = jnp.where(lane < 64, turned[64:], corner)


def call(body, outs, specs, flops=0, moved=0, name=None):
    return pl.pallas_call(
        body,
        out_shape=[jax.ShapeDtypeStruct(shape, dtype) for shape, dtype in outs],
        in_specs=specs,
        out_specs=[VMEM] * len(outs),
        compiler_params=pltpu.CompilerParams(vmem_limit_bytes=40 << 20),
        cost_estimate=pl.CostEstimate(flops=flops, bytes_accessed=moved, transcendentals=0),
        name=name,
    )


def local(queries, keyval, keep, lists):
    bf16, f32 = jnp.bfloat16, jnp.float32
    lats, lons = lax.axis_size("lat"), lax.axis_size("lon")
    up = [(i, i + 1) for i in range(lats - 1)]
    down = [(i + 1, i) for i in range(lats - 1)]
    east = [(i, (i + 1) % lons) for i in range(lons)]
    west = [(i, (i - 1) % lons) for i in range(lons)]
    edge = ((HEADS + 1, 2 * BLOCK, HD), bf16)

    low = lax.ppermute(keyval, "lat", up)
    high = lax.ppermute(keyval, "lat", down)
    lat = lax.axis_index("lat").astype(jnp.int32).reshape(1)
    to_west, to_east, seen = call(
        functools.partial(prepare_body, 2 * lats),
        [edge, edge, ((2, 2 * BLOCK, 128), bf16)],
        [SMEM, SMEM, SMEM, VMEM],
        moved=1 << 20,
        name="prepare",
    )(lat, keep, lists, queries)
    from_west = lax.ppermute(to_east, "lon", east)
    from_east = lax.ppermute(to_west, "lon", west)
    back_west, back_east = call(
        remote_body, [edge, edge], [VMEM] * 5, flops=1 << 29, moved=4 << 20, name="remote"
    )(from_west, from_east, low, keyval, high)
    part_east = lax.ppermute(back_west, "lon", west)
    part_west = lax.ppermute(back_east, "lon", east)
    own, level = call(
        own_body,
        [((HEADS, 4 * BLOCK, HD), bf16), ((4 * BLOCK, 128), f32)],
        [VMEM] * 5,
        flops=1 << 30,
        moved=4 << 20,
        name="own",
    )(queries, seen, low, keyval, high)
    attended, packed = call(
        combine_body,
        [(queries.shape, bf16), ((2 * HEADS, ROWS, 128), bf16)],
        [VMEM] * 4,
        name="combine",
    )(own, level, part_west, part_east)
    swapped = lax.all_to_all(packed, "lon", 0, 0, tiled=True)
    (summed,) = call(sum_body, [((2 * HEADS, ROWS, 128), bf16)], [VMEM], name="total")(swapped)
    gathered = lax.all_to_all(summed, "lon", 0, 0, tiled=True)
    (gram,) = call(unpack_body, [((1, HEADS, HD, HD), f32)], [VMEM], name="unpack")(gathered)
    return attended, gram


def solution(mesh):
    placed = (P("lat", "lon", None), P(None, "lat", "lon", None), P(), P("lat", "lon", None))
    return jax.shard_map(
        local,
        mesh=mesh,
        in_specs=placed,
        out_specs=(P("lat", "lon", None), P("lat", None, None, None)),
        check_vma=False,
    )
```

time: 293 us -> 98.8 us (0.34)
  the two profiles are of different devices: /device:TPU:64 before, /device:TPU:8 now
where the time goes in v1:
time: 98.8 us; the launch traced here: 98.4 us
  blocking collectives  49.9 us (51%)
  starting transfers between devices  19.5 us (20%)
  Pallas kernels  18.5 us (19%)
  waiting for transfers between devices  6.8 us (7%)
  local copies, waits for them, and re-layouts  2.94 us (3%)
    all_to_all x1, blocking collectives, local(): swapped = lax.all_to_all(packed, 'lon', 0, 0, tiled=True)  33 us
    all_to_all x1, blocking collectives, local(): gathered = lax.all_to_all(summed, 'lon', 0, 0, tiled=True)  16.9 us
    pallas_call x1, Pallas kernels, local(): call(remote_body, [edge, edge], [VMEM] * 5, flops=1 << 29, moved=4 << 20,...  8.38 us
    ppermute x1, starting transfers between devices, local(): part_east = lax.ppermute(back_west, 'lon', west)  5.18 us
    ppermute x1, starting transfers between devices, local(): from_east = lax.ppermute(to_west, 'lon', west)  4.55 us
    pallas_call x1, Pallas kernels, local(): call(own_body, [((HEADS, 4 * BLOCK, HD), bf16), ((4 * BLOCK, 128), f32)],...  4.32 us
    pallas_call x1, Pallas kernels, local(): call(combine_body, [(queries.shape, bf16), ((2 * HEADS, ROWS, 128), bf16)...  3.69 us
    ppermute x1, starting transfers between devices, local(): from_west = lax.ppermute(to_east, 'lon', east)  3.4 us
  transfers between devices with their start and end apart: 6, of which 3 were waited for; matrix products, arithmetic and copies ran while one was open for 0% of the time, Pallas kernels for 5%

profile of v1, /device:TPU:8, one launch (start us, length us, event | category | flops | bytes accessed | tf_op | source)
XLA Modules:
  0.0 98.4 jit_solution(9140208870142408852)
XLA Ops:
  0.6 1.8 %collective-permute-start = (bf16[2,2,64,2048]{3,2,1,0:T(8,128)(2,1)}, bf16[2,2,64,2048]{3,2,1,0:T(8,128)(2,1)S(1)}, u32[]{:S(2)}, u32[]{:S(2)}) collective-permute-start(bf16[2,2,64,2048]{3,2,1,0:T(8,128)(2,1)} %own_ref.3), channel_id=1, source_target_pairs={{0,32},{32,64},{64,96},{96,128},{128,160},{160,192},{192,224},{224... | collective-permute-start | bytes 3145736 | tf_op jit(solution)/shard_map/ppermute | solution.py:210
  2.4 1.3 %collective-permute-start.1 = (bf16[2,2,64,2048]{3,2,1,0:T(8,128)(2,1)}, bf16[2,2,64,2048]{3,2,1,0:T(8,128)(2,1)S(1)}, u32[]{:S(2)}, u32[]{:S(2)}) collective-permute-start(bf16[2,2,64,2048]{3,2,1,0:T(8,128)(2,1)} %own_ref.3), channel_id=1, source_target_pairs={{32,0},{64,32},{96,64},{128,96},{160,128},{192,160},{224,192},{256... | collective-permute-start | bytes 3145736 | tf_op jit(solution)/shard_map/ppermute | solution.py:211
  3.8 0.0 copy-start.4
  3.8 0.0 copy-start.5
  3.8 0.7 copy-done.4
  4.4 0.0 copy-done.5
  4.4 0.0 copy-start.2
  4.4 1.0 %copy-done.2 = bf16[2,64,2048]{2,1,0:T(8,128)(2,1)S(1)} copy-done((bf16[2,64,2048]{2,1,0:T(8,128)(2,1)S(1)}, bf16[2,64,2048]{2,1,0:T(8,128)(2,1)}, u32[]{:S(2)}) %copy-start.2) | copy-done | bytes 524312
  5.5 0.0 copy-start.3
  5.5 0.7 prepare.1
  6.2 3.4 %collective-permute-start.2 = (bf16[17,64,128]{2,1,0:T(8,128)(2,1)S(1)}, bf16[17,64,128]{2,1,0:T(8,128)(2,1)S(1)}, u32[]{:S(2)}, u32[]{:S(2)}) collective-permute-start(bf16[17,64,128]{2,1,0:T(8,128)(2,1)S(1)} %get-tuple-element.14), channel_id=1, source_target_pairs={{0,1},{1,2},{2,3},{3,4},{4,5},{5,6},{6,7},{7,8},{8,9},{9,10},{10,1... | collective-permute-start | bytes 835592 | tf_op jit(solution)/shard_map/ppermute | solution.py:220
  9.6 4.6 %collective-permute-start.3 = (bf16[17,64,128]{2,1,0:T(8,128)(2,1)S(1)}, bf16[17,64,128]{2,1,0:T(8,128)(2,1)S(1)}, u32[]{:S(2)}, u32[]{:S(2)}) collective-permute-start(bf16[17,64,128]{2,1,0:T(8,128)(2,1)S(1)} %get-tuple-element.15), channel_id=1, source_target_pairs={{0,31},{1,0},{2,1},{3,2},{4,3},{5,4},{6,5},{7,6},{8,7},{9,8},{10,9... | collective-permute-start | bytes 835592 | tf_op jit(solution)/shard_map/ppermute | solution.py:221
  14.1 3.2 %collective-permute-done.2.west_ref = bf16[17,64,128]{2,1,0:T(8,128)(2,1)S(1)} collective-permute-done((bf16[17,64,128]{2,1,0:T(8,128)(2,1)S(1)}, bf16[17,64,128]{2,1,0:T(8,128)(2,1)S(1)}, u32[]{:S(2)}, u32[]{:S(2)}) %collective-permute-start.2) | collective-permute-done | bytes 278560 | tf_op jit(solution)/shard_map/ppermute | solution.py:220
  17.4 1.7 %collective-permute-done.3.east_ref = bf16[17,64,128]{2,1,0:T(8,128)(2,1)S(1)} collective-permute-done((bf16[17,64,128]{2,1,0:T(8,128)(2,1)S(1)}, bf16[17,64,128]{2,1,0:T(8,128)(2,1)S(1)}, u32[]{:S(2)}, u32[]{:S(2)}) %collective-permute-start.3) | collective-permute-done | bytes 278560 | tf_op jit(solution)/shard_map/ppermute | solution.py:221
  19.1 0.0 collective-permute-done.low_ref
  19.1 0.0 collective-permute-done.1.high_ref
  19.1 0.0 copy-start
  19.1 1.2 %copy-done = bf16[2,2,64,2048]{3,2,1,0:T(8,128)(2,1)S(1)} copy-done((bf16[2,2,64,2048]{3,2,1,0:T(8,128)(2,1)S(1)}, bf16[2,2,64,2048]{3,2,1,0:T(8,128)(2,1)}, u32[]{:S(2)}) %copy-start) | copy-done | bytes 1048600
  20.4 0.0 copy-start.1
  20.4 8.4 %remote.1 = (bf16[17,64,128]{2,1,0:T(8,128)(2,1)S(1)}, bf16[17,64,128]{2,1,0:T(8,128)(2,1)S(1)}) custom-call(bf16[17,64,128]{2,1,0:T(8,128)(2,1)S(1)} %collective-permute-done.2.west_ref, bf16[17,64,128]{2,1,0:T(8,128)(2,1)S(1)} %collective-permute-done.3.east_ref, bf16[2,2,64,2048]{3,2,1,0:T(8,128)(2,1)S(1)} %collective-permute-done.low_ref, ...), custom_call_target="tpu_custom_call" | custom-call | flops 536870912 | bytes 4194304 | tf_op jit(solution)/shard_map/remote/pallas_call | solution.py:222
  28.7 3.2 %collective-permute-start.4 = (bf16[17,64,128]{2,1,0:T(8,128)(2,1)S(1)}, bf16[17,64,128]{2,1,0:T(8,128)(2,1)S(1)}, u32[]{:S(2)}, u32[]{:S(2)}) collective-permute-start(bf16[17,64,128]{2,1,0:T(8,128)(2,1)S(1)} %get-tuple-element.16), channel_id=1, source_target_pairs={{0,1},{1,2},{2,3},{3,4},{4,5},{5,6},{6,7},{7,8},{8,9},{9,10},{10,1... | collective-permute-start | bytes 835592 | tf_op jit(solution)/shard_map/ppermute | solution.py:226
  32.0 5.2 %collective-permute-start.5 = (bf16[17,64,128]{2,1,0:T(8,128)(2,1)S(1)}, bf16[17,64,128]{2,1,0:T(8,128)(2,1)S(1)}, u32[]{:S(2)}, u32[]{:S(2)}) collective-permute-start(bf16[17,64,128]{2,1,0:T(8,128)(2,1)S(1)} %get-tuple-element.17), channel_id=1, source_target_pairs={{0,31},{1,0},{2,1},{3,2},{4,3},{5,4},{6,5},{7,6},{8,7},{9,8},{10,9... | collective-permute-start | bytes 835592 | tf_op jit(solution)/shard_map/ppermute | solution.py:225
  37.2 0.0 copy-done.3
  37.2 0.0 copy-done.1
  37.2 4.3 %own.1 = (bf16[16,128,128]{2,1,0:T(8,128)(2,1)S(1)}, f32[128,128]{1,0:T(8,128)S(1)}) custom-call(bf16[2,64,2048]{2,1,0:T(8,128)(2,1)S(1)} %copy-done.3, bf16[2,64,128]{2,1,0:T(8,128)(2,1)S(1)} %get-tuple-element.11.seen_ref, bf16[2,2,64,2048]{3,2,1,0:T(8,128)(2,1)S(1)} %collective-permute-done.low_ref, bf16[2,2,64,2048]{3,2,1,0:T(8,128)(2,1)S(1)} %copy-done.1, ...), custom_call_target="tpu_custom_call" | custom-call | flops 1073741824 | bytes 4194304 | tf_op jit(solution)/shard_map/own/pallas_call | solution.py:227
  41.5 0.0 collective-permute-done.4.west_ref
  41.6 1.8 %collective-permute-done.5.east_ref = bf16[17,64,128]{2,1,0:T(8,128)(2,1)S(1)} collective-permute-done((bf16[17,64,128]{2,1,0:T(8,128)(2,1)S(1)}, bf16[17,64,128]{2,1,0:T(8,128)(2,1)S(1)}, u32[]{:S(2)}, u32[]{:S(2)}) %collective-permute-start.5) | collective-permute-done | bytes 278560 | tf_op jit(solution)/shard_map/ppermute | solution.py:225
  43.3 3.7 %combine.1 = (bf16[2,64,2048]{2,1,0:T(8,128)(2,1)}, bf16[32,40,128]{2,1,0:T(8,128)(2,1)S(1)}) custom-call(bf16[16,128,128]{2,1,0:T(8,128)(2,1)S(1)} %get-tuple-element.12.own_ref, f32[128,128]{1,0:T(8,128)S(1)} %get-tuple-element.13.level_ref, bf16[17,64,128]{2,1,0:T(8,128)(2,1)S(1)} %collective-permute-done.4.west_ref, ...), custom_call_target="tpu_custom_call" | custom-call | tf_op jit(solution)/shard_map/combine/pallas_call | solution.py:235
  47.0 33.0 %all_to_all.10.x_ref = bf16[32,40,128]{2,1,0:T(8,128)(2,1)S(1)} all-to-all(bf16[32,40,128]{2,1,0:T(8,128)(2,1)S(1)} %get-tuple-element.19), channel_id=1, replica_groups=mesh['lat'=24,'lon'=32] {'lon'}, dimensions={0} | all-to-all | bytes 655360 | tf_op jit(solution)/shard_map/all_to_all | solution.py:241
  80.0 0.1 total.1
  80.1 16.9 %all_to_all.11.x_ref = bf16[32,40,128]{2,1,0:T(8,128)(2,1)S(1)} all-to-all(bf16[32,40,128]{2,1,0:T(8,128)(2,1)S(1)} %total.1), channel_id=1, replica_groups=mesh['lat'=24,'lon'=32] {'lon'}, dimensions={0} | all-to-all | bytes 655360 | tf_op jit(solution)/shard_map/all_to_all | solution.py:243
  97.0 1.4 %unpack.1 = f32[1,16,128,128]{3,2,1,0:T(8,128)} custom-call(bf16[32,40,128]{2,1,0:T(8,128)(2,1)S(1)} %all_to_all.11.x_ref), custom_call_target="tpu_custom_call" | custom-call | tf_op jit(solution)/shard_map/unpack/pallas_call | solution.py:244
Async XLA Ops:
  0.6 18.5 %collective-permute-start = (bf16[2,2,64,2048]{3,2,1,0:T(8,128)(2,1)}, bf16[2,2,64,2048]{3,2,1,0:T(8,128)(2,1)S(1)}, u32[]{:S(2)}, u32[]{:S(2)}) collective-permute-start(bf16[2,2,64,2048]{3,2,1,0:T(8,128)(2,1)} %own_ref.3), channel_id=1, source_target_pairs={{0,32},{32,64},{64,96},{96,128},{128,160},{160,192},{192,224},{224... | collective-permute-start | bytes 3145736 | tf_op jit(solution)/shard_map/ppermute | solution.py:210
  2.4 16.7 %collective-permute-start.1 = (bf16[2,2,64,2048]{3,2,1,0:T(8,128)(2,1)}, bf16[2,2,64,2048]{3,2,1,0:T(8,128)(2,1)S(1)}, u32[]{:S(2)}, u32[]{:S(2)}) collective-permute-start(bf16[2,2,64,2048]{3,2,1,0:T(8,128)(2,1)} %own_ref.3), channel_id=1, source_target_pairs={{32,0},{64,32},{96,64},{128,96},{160,128},{192,160},{224,192},{256... | collective-permute-start | bytes 3145736 | tf_op jit(solution)/shard_map/ppermute | solution.py:211
  3.8 0.7 copy-start.4
  3.8 0.7 copy-start.5
  4.4 1.0 %copy-start.2 = (bf16[2,64,2048]{2,1,0:T(8,128)(2,1)S(1)}, bf16[2,64,2048]{2,1,0:T(8,128)(2,1)}, u32[]{:S(2)}) copy-start(bf16[2,64,2048]{2,1,0:T(8,128)(2,1)} %q_ref.3) | copy-start | bytes 1572868
  5.5 31.7 %copy-start.3 = (bf16[2,64,2048]{2,1,0:T(8,128)(2,1)S(1)}, bf16[2,64,2048]{2,1,0:T(8,128)(2,1)}, u32[]{:S(2)}) copy-start(bf16[2,64,2048]{2,1,0:T(8,128)(2,1)} %q_ref.3) | copy-start | bytes 1572868
  6.2 11.2 %collective-permute-start.2 = (bf16[17,64,128]{2,1,0:T(8,128)(2,1)S(1)}, bf16[17,64,128]{2,1,0:T(8,128)(2,1)S(1)}, u32[]{:S(2)}, u32[]{:S(2)}) collective-permute-start(bf16[17,64,128]{2,1,0:T(8,128)(2,1)S(1)} %get-tuple-element.14), channel_id=1, source_target_pairs={{0,1},{1,2},{2,3},{3,4},{4,5},{5,6},{6,7},{7,8},{8,9},{9,10},{10,1... | collective-permute-start | bytes 835592 | tf_op jit(solution)/shard_map/ppermute | solution.py:220
  9.6 9.5 %collective-permute-start.3 = (bf16[17,64,128]{2,1,0:T(8,128)(2,1)S(1)}, bf16[17,64,128]{2,1,0:T(8,128)(2,1)S(1)}, u32[]{:S(2)}, u32[]{:S(2)}) collective-permute-start(bf16[17,64,128]{2,1,0:T(8,128)(2,1)S(1)} %get-tuple-element.15), channel_id=1, source_target_pairs={{0,31},{1,0},{2,1},{3,2},{4,3},{5,4},{6,5},{7,6},{8,7},{9,8},{10,9... | collective-permute-start | bytes 835592 | tf_op jit(solution)/shard_map/ppermute | solution.py:221
  19.1 1.2 %copy-start = (bf16[2,2,64,2048]{3,2,1,0:T(8,128)(2,1)S(1)}, bf16[2,2,64,2048]{3,2,1,0:T(8,128)(2,1)}, u32[]{:S(2)}) copy-start(bf16[2,2,64,2048]{3,2,1,0:T(8,128)(2,1)} %own_ref.3) | copy-start | bytes 3145732
  20.4 16.8 %copy-start.1 = (bf16[2,2,64,2048]{3,2,1,0:T(8,128)(2,1)S(1)}, bf16[2,2,64,2048]{3,2,1,0:T(8,128)(2,1)}, u32[]{:S(2)}) copy-start(bf16[2,2,64,2048]{3,2,1,0:T(8,128)(2,1)} %own_ref.3) | copy-start | bytes 3145732
  28.7 12.8 %collective-permute-start.4 = (bf16[17,64,128]{2,1,0:T(8,128)(2,1)S(1)}, bf16[17,64,128]{2,1,0:T(8,128)(2,1)S(1)}, u32[]{:S(2)}, u32[]{:S(2)}) collective-permute-start(bf16[17,64,128]{2,1,0:T(8,128)(2,1)S(1)} %get-tuple-element.16), channel_id=1, source_target_pairs={{0,1},{1,2},{2,3},{3,4},{4,5},{5,6},{6,7},{7,8},{8,9},{9,10},{10,1... | collective-permute-start | bytes 835592 | tf_op jit(solution)/shard_map/ppermute | solution.py:226
  32.0 11.3 %collective-permute-start.5 = (bf16[17,64,128]{2,1,0:T(8,128)(2,1)S(1)}, bf16[17,64,128]{2,1,0:T(8,128)(2,1)S(1)}, u32[]{:S(2)}, u32[]{:S(2)}) collective-permute-start(bf16[17,64,128]{2,1,0:T(8,128)(2,1)S(1)} %get-tuple-element.17), channel_id=1, source_target_pairs={{0,31},{1,0},{2,1},{3,2},{4,3},{5,4},{6,5},{7,6},{8,7},{9,8},{10,9... | collective-permute-start | bytes 835592 | tf_op jit(solution)/shard_map/ppermute | solution.py:225

commit v2 on v1

v2 whole, which is shorter than its diff:
```python
import functools

import jax
import jax.numpy as jnp
from jax import lax
from jax.experimental import pallas as pl
from jax.experimental.pallas import tpu as pltpu
from jax.sharding import PartitionSpec as P

HEADS = 16
HD = 128
BLOCK = 32
HALO = 2
CAND = 15
NB = 13
ROWS = 40
NEG = -1e30
LOG2 = 1.4426950408889634 * HD ** (-0.5)

VMEM = pl.BlockSpec(memory_space=pltpu.VMEM)
SMEM = pl.BlockSpec(memory_space=pltpu.SMEM)
HBM = pl.BlockSpec(memory_space=pltpu.HBM)
ANY = pl.BlockSpec(memory_space=pl.ANY)


def iota(shape, axis):
    return lax.broadcasted_iota(jnp.int32, shape, axis)


def place(lat_ref, lon_ref):
    return lax.rem(lat_ref[0], 2), lax.rem(lon_ref[0], 2)


def prepare_body(rows_total, lat_ref, lon_ref, keep_hbm, lists_hbm, q_hbm, out0_ref, out1_ref, keep_ref, lists_ref, q_ref, sems):
    copies = [
        pltpu.make_async_copy(src, dst, sems.at[i])
        for i, (src, dst) in enumerate(((lists_hbm, lists_ref), (keep_hbm, keep_ref), (q_hbm, q_ref)))
    ]
    for copy in copies:
        copy.start()
    first = lat_ref[0] * 2
    _, odd = place(lat_ref, lon_ref)
    lane = iota((1, 128), 1)
    copies[0].wait()
    copies[1].wait()
    for b, out in ((1 - odd, out0_ref), (odd, out1_ref)):
        for t in range(2):
            listed = jnp.zeros((1, 128), jnp.int32)
            for n in range(NB):
                listed = jnp.where(lane == lists_ref[t, b, n], 1, listed)
            usable = jnp.zeros((1, 128), jnp.int32)
            for k in range(2 * HALO + 1):
                row = first + (t + k - HALO)
                inside = jnp.logical_and(row >= 0, row < rows_total)
                if k == HALO:
                    good = 1
                else:
                    good = jnp.where(inside, keep_ref[jnp.clip(row, 0, rows_total - 1)], 0)
                usable = jnp.where((lane >= 3 * k) & (lane < 3 * k + 3), good, usable)
            seen = jnp.where((listed == 1) & (usable == 1), 1.0, 0.0)
            seen = jnp.broadcast_to(seen, (BLOCK, 128)).astype(jnp.bfloat16)
            out[HEADS, t * BLOCK : (t + 1) * BLOCK, :] = seen
    copies[2].wait()
    for b, out in ((1 - odd, out0_ref), (odd, out1_ref)):
        cells = pl.ds(pl.multiple_of(b * BLOCK, BLOCK), BLOCK)
        for t in range(2):
            for h in range(HEADS):
                out[h, t * BLOCK : (t + 1) * BLOCK, :] = q_ref[t, cells, h * HD : (h + 1) * HD]


def hold_body(x_ref, after_ref, out_ref):
    del after_ref
    out_ref[...] = x_ref[...]


def bias_of(seen, t, lat_odd, blocks, step):
    shape = (128, 6 * blocks * BLOCK)
    cand, key = iota(shape, 0), iota(shape, 1)
    slot = key // (blocks * BLOCK)
    row = slot + jnp.where(slot < 2, 4 * lat_odd, jnp.where(slot < 4, 0, -4 * lat_odd)) - t
    step = step + (key // BLOCK) % blocks
    inside = (row >= 0) & (row <= 2 * HALO) & (step >= -1) & (step <= 1)
    spread = jnp.where(inside & (cand == 3 * row + step + 1), 1.0, 0.0).astype(jnp.bfloat16)
    shown = jnp.dot(seen, spread, preferred_element_type=jnp.float32)
    return jnp.where(shown > 0.5, 0.0, NEG)


def rows_of(refs, part, cells, h):
    return jnp.concatenate(
        [ref[part, r, cells, h * HD : (h + 1) * HD] for ref in refs for r in range(2)], axis=0
    )


def scores_of(q, keys):
    return lax.dot_general(q, keys, (((1,), (1,)), ((), ())), preferred_element_type=jnp.float32)


def staged(*stages):
    held = [{} for _ in stages]
    for step in range(HEADS + len(stages) - 1):
        for i, stage in enumerate(stages):
            h = step - i
            if 0 <= h < HEADS:
                held[i][h] = stage(h) if i == 0 else stage(h, held[i - 1].pop(h))


def softmax_stage(bias, stats):
    lane = iota(bias.shape[:1] + (128,), 1)

    def stage(h, scores):
        scores = scores * LOG2 + bias
        top = jnp.max(scores, axis=-1, keepdims=True)
        weights = jnp.exp2(scores - top)
        total = jnp.sum(weights, axis=-1, keepdims=True)
        stats[0] = jnp.where(lane == h, top, stats[0])
        stats[1] = jnp.where(lane == h, total, stats[1])
        return weights.astype(jnp.bfloat16)

    return stage


def own_body(lat_ref, lon_ref, q0_ref, q1_ref, far_ref, own_ref, near_ref, after_ref, out_ref, top_ref, total_ref):
    del after_ref
    refs = (far_ref, own_ref, near_ref)
    lat_odd, odd = place(lat_ref, lon_ref)
    cells = slice(0, 2 * BLOCK)
    bias = jnp.concatenate(
        [
            bias_of(ref[HEADS, t * BLOCK : (t + 1) * BLOCK, :], t, lat_odd, 2, -b)
            for b, ref in ((1 - odd, q0_ref), (odd, q1_ref))
            for t in range(2)
        ],
        axis=0,
    )
    stats = [jnp.zeros((4 * BLOCK, 128), jnp.float32), jnp.ones((4 * BLOCK, 128), jnp.float32)]

    def score(h):
        return scores_of(jnp.concatenate([q0_ref[h], q1_ref[h]], axis=0), rows_of(refs, 0, cells, h))

    def mix(h, weights):
        mixed = jnp.dot(weights, rows_of(refs, 1, cells, h), preferred_element_type=jnp.float32)
        out_ref[h] = mixed.astype(jnp.bfloat16)

    staged(score, softmax_stage(bias, stats), mix)
    top_ref[...] = stats[0]
    total_ref[...] = stats[1]


def thirds(x):
    coarse = x.astype(jnp.bfloat16).astype(jnp.float32)
    rest = x - coarse
    middle = rest.astype(jnp.bfloat16).astype(jnp.float32)
    return coarse, middle, rest - middle


def remote_body(partner, lat_ref, lon_ref, q_ref, far_ref, own_ref, near_ref, out_ref):
    refs = (far_ref, own_ref, near_ref)
    lat_odd, odd = place(lat_ref, lon_ref)
    held = 1 - odd if partner == 0 else odd
    cells = pl.ds(pl.multiple_of(held * BLOCK, BLOCK), BLOCK)
    bias = jnp.concatenate(
        [
            bias_of(q_ref[HEADS, t * BLOCK : (t + 1) * BLOCK, :], t, lat_odd, 1, 1 - 2 * held)
            for t in range(2)
        ],
        axis=0,
    )
    stats = [jnp.zeros((2 * BLOCK, 128), jnp.float32), jnp.ones((2 * BLOCK, 128), jnp.float32)]

    def score(h):
        return scores_of(q_ref[h], rows_of(refs, 0, cells, h))

    def mix(h, weights):
        mixed = jnp.dot(weights, rows_of(refs, 1, cells, h), preferred_element_type=jnp.float32)
        out_ref[h] = mixed.astype(jnp.bfloat16)

    staged(score, softmax_stage(bias, stats), mix)
    lane = iota((2 * BLOCK, 128), 1)
    packed = jnp.zeros((2 * BLOCK, 128), jnp.float32)
    for i, part in enumerate(thirds(stats[0]) + thirds(stats[1])):
        part = jnp.where(lane < HEADS, part, 0.0)
        packed = packed + (pltpu.roll(part, i * HEADS, 1) if i else part)
    out_ref[HEADS] = packed.astype(jnp.bfloat16)


def combine_body(lon_ref, own_ref, top_ref, total_ref, part0_ref, part1_ref, out_ref, packed_ref):
    half = 2 * BLOCK
    odd = lax.rem(lon_ref[0], 2)
    split = jnp.concatenate([part0_ref[HEADS], part1_ref[HEADS]], axis=0).astype(jnp.float32)
    moved = [split] + [pltpu.roll(split, 128 - i * HEADS, 1) for i in range(1, 6)]
    far_top = moved[0] + moved[1] + moved[2]
    far_total = moved[3] + moved[4] + moved[5]
    lane = iota((4 * BLOCK, 128), 1)
    far_top = jnp.where(lane < HEADS, far_top, 0.0)
    far_total = jnp.where(lane < HEADS, far_total, 1.0)
    near_top = top_ref[...]
    top = jnp.maximum(near_top, far_top)
    mine, theirs = jnp.exp2(near_top - top), jnp.exp2(far_top - top)
    inverse = 1.0 / (mine * total_ref[...] + theirs * far_total)
    mine, theirs = mine * inverse, theirs * inverse
    row, lane = iota((64, 128), 0), iota((64, 128), 1)

    def merge(h):
        far = jnp.concatenate([part0_ref[h], part1_ref[h]], axis=0).astype(jnp.float32)
        near = own_ref[h].astype(jnp.float32)
        cells = (near * mine[:, h : h + 1] + far * theirs[:, h : h + 1]).astype(jnp.bfloat16)
        for i, b in enumerate((1 - odd, odd)):
            place_b = pl.ds(pl.multiple_of(b * BLOCK, BLOCK), BLOCK)
            for t in range(2):
                low = i * half + t * BLOCK
                out_ref[t, place_b, h * HD : (h + 1) * HD] = cells[low : low + BLOCK]
        return cells

    def multiply(h, cells):
        return lax.dot_general(cells, cells, (((0,), (0,)), ((), ())), preferred_element_type=jnp.float32)

    def pack(h, gram):
        upper, lower = gram[:64], gram[64:]
        folded = jnp.where((lane < 64) & (row > lane), pltpu.roll(lower, 64, 1), upper).astype(jnp.bfloat16)
        diagonal = jnp.sum(jnp.where(lane - 64 == row, lower, 0.0), axis=0, keepdims=True)
        diagonal = jnp.broadcast_to(diagonal, (8, 128)).astype(jnp.bfloat16)
        for part in range(2):
            packed_ref[2 * h + part, :32, :] = folded[part * 32 : (part + 1) * 32]
            packed_ref[2 * h + part, 32:, :] = diagonal

    staged(merge, multiply, pack)


def sum_body(x_ref, out_ref):
    total = jnp.sum(x_ref[...].astype(jnp.float32), axis=0).astype(jnp.bfloat16)
    out_ref[...] = jnp.broadcast_to(total[None], out_ref.shape)


def unpack_body(x_ref, out_ref):
    row, lane = iota((64, 128), 0), iota((64, 128), 1)
    for h in range(HEADS):
        folded = jnp.concatenate([x_ref[2 * h, :32, :], x_ref[2 * h + 1, :32, :]], axis=0).astype(jnp.float32)
        diagonal = x_ref[2 * h, 32:, :].astype(jnp.float32)[:1]
        turned = jnp.concatenate([folded, jnp.zeros_like(folded)], axis=0).T
        out_ref[0, h, :64, :] = jnp.where((lane < 64) & (row > lane), turned[:64], folded)
        corner = pltpu.roll(jnp.where(row > lane, folded, turned[:64]), 64, 1)
        corner = jnp.where(lane - 64 == row, diagonal, corner)
        out_ref[0, h, 64:, :] = jnp.where(lane < 64, turned[64:], corner)


def call(body, outs, specs, flops=0, moved=0, name=None, scratch=()):
    return pl.pallas_call(
        body,
        out_shape=[jax.ShapeDtypeStruct(shape, dtype) for shape, dtype in outs],
        in_specs=specs,
        out_specs=[VMEM] * len(outs),
        scratch_shapes=scratch,
        compiler_params=pltpu.CompilerParams(vmem_limit_bytes=40 << 20),
        cost_estimate=pl.CostEstimate(flops=flops, bytes_accessed=moved, transcendentals=0),
        name=name,
    )


def local(queries, keyval, keep, lists):
    bf16, f32 = jnp.bfloat16, jnp.float32
    lats, lons = lax.axis_size("lat"), lax.axis_size("lon")
    chips = [(i, i + 1 if i % 2 else i - 1) for i in range(1, lats - 1)]
    cores = [(i, i ^ 1) for i in range(lats)]
    pairs = [(i, i ^ 1) for i in range(lons)], [(i, (i + (1 if i % 2 else -1)) % lons) for i in range(lons)]
    edge = ((HEADS + 1, 2 * BLOCK, HD), bf16)
    level = ((4 * BLOCK, 128), f32)

    far = lax.ppermute(keyval, "lat", chips)
    near = lax.ppermute(keyval, "lat", cores)
    lat = lax.axis_index("lat").astype(jnp.int32).reshape(1)
    lon = lax.axis_index("lon").astype(jnp.int32).reshape(1)
    mine = call(
        functools.partial(prepare_body, 2 * lats),
        [edge, edge],
        [SMEM, SMEM, HBM, HBM, HBM],
        moved=1 << 20,
        name="prepare",
        scratch=[
            pltpu.SMEM(keep.shape, jnp.int32),
            pltpu.SMEM(lists.shape, jnp.int32),
            pltpu.VMEM(queries.shape, bf16),
            pltpu.SemaphoreType.DMA((3,)),
        ],
    )(lat, lon, keep, lists, queries)
    theirs = [lax.ppermute(x, "lon", pair) for x, pair in zip(mine, pairs)]
    (held,) = call(hold_body, [(keyval.shape, bf16)], [VMEM, ANY], moved=2 << 20, name="hold")(keyval, mine[0])
    answers = [
        call(
            functools.partial(remote_body, i),
            [edge],
            [SMEM, SMEM] + [VMEM] * 4,
            flops=1 << 28,
            moved=4 << 20,
            name=f"remote{i}",
        )(lat, lon, theirs[i], far, held, near)[0]
        for i in range(2)
    ]
    parts = [lax.ppermute(x, "lon", pair) for x, pair in zip(answers, pairs)]
    own, top, total = call(
        own_body,
        [((HEADS, 4 * BLOCK, HD), bf16), level, level],
        [SMEM, SMEM] + [VMEM] * 5 + [ANY],
        flops=1 << 29,
        moved=4 << 20,
        name="own",
    )(lat, lon, *mine, far, held, near, answers[1])
    attended, packed = call(
        combine_body,
        [(queries.shape, bf16), ((2 * HEADS, ROWS, 128), bf16)],
        [SMEM] + [VMEM] * 5,
        name="combine",
    )(lon, own, top, total, *parts)
    swapped = lax.all_to_all(packed, "lon", 0, 0, tiled=True)
    (summed,) = call(sum_body, [((2 * HEADS, ROWS, 128), bf16)], [VMEM], name="total")(swapped)
    gathered = lax.all_to_all(summed, "lon", 0, 0, tiled=True)
    (gram,) = call(unpack_body, [((1, HEADS, HD, HD), f32)], [VMEM], name="unpack")(gathered)
    return attended, gram


def solution(mesh):
    placed = (P("lat", "lon", None), P(None, "lat", "lon", None), P(), P("lat", "lon", None))
    return jax.shard_map(
        local,
        mesh=mesh,
        in_specs=placed,
        out_specs=(P("lat", "lon", None), P("lat", None, None, None)),
        check_vma=False,
    )
```

time: 98.8 us -> 83.3 us (0.84)
  blocking collectives: 49.9 us -> 40.5 us
  Pallas kernels: 18.5 us -> 10.3 us
  starting transfers between devices: 19.5 us -> 22 us
    all_to_all x1, blocking collectives: 33 us -> 23.7 us  [local(): swapped = lax.all_to_all(packed, 'lon', 0, 0, tiled=True)]
    pallas_call x3 -> x5, Pallas kernels: 13.4 us -> 6.46 us  [the longest x2 3.71 us: local(): call(functools.partial(remote_body, i), [edge], [SMEM, SMEM] + [VMEM] * 4...]
    ppermute x6, starting transfers between devices: 19.5 us -> 22 us  [the longest x2 8.39 us: local(): parts = [lax.ppermute(x, 'lon', pair) for x, pair in zip(answers, pairs)]]
    pallas_call x1, Pallas kernels: 3.69 us -> 2.39 us  [local(): call(combine_body, [(queries.shape, bf16), ((2 * HEADS, ROWS, 128), bf16)...]
    unnamed x12 -> x8, local copies, waits for them, and re-layouts: 2.94 us -> 2.93 us
  transfers between devices with their start and end apart: 6 -> 6, of which waited for: 3 -> 2; matrix products, arithmetic and copies ran while one was open for 0% -> 0% of each run, Pallas kernels for 5% -> 8%
where the time goes in v2:
time: 83.3 us; the launch traced here: 82.8 us
  blocking collectives  40.5 us (49%)
  starting transfers between devices  22 us (26%)
  Pallas kernels  10.3 us (12%)
  waiting for transfers between devices  6.38 us (8%)
  local copies, waits for them, and re-layouts  2.93 us (4%)
    all_to_all x1, blocking collectives, local(): swapped = lax.all_to_all(packed, 'lon', 0, 0, tiled=True)  23.7 us
    all_to_all x1, blocking collectives, local(): gathered = lax.all_to_all(summed, 'lon', 0, 0, tiled=True)  16.8 us
    ppermute x2, starting transfers between devices, local(): parts = [lax.ppermute(x, 'lon', pair) for x, pair in zip(answers, pairs)]  8.39 us
    ppermute x2, starting transfers between devices, local(): theirs = [lax.ppermute(x, 'lon', pair) for x, pair in zip(mine, pairs)]  7.29 us
    ppermute x1, starting transfers between devices, local(): near = lax.ppermute(keyval, 'lat', cores)  5.58 us
    ppermute x2, waiting for transfers between devices, local(): parts = [lax.ppermute(x, 'lon', pair) for x, pair in zip(answers, pairs)]  4.51 us
    pallas_call x2, Pallas kernels, local(): call(functools.partial(remote_body, i), [edge], [SMEM, SMEM] + [VMEM] * 4...  3.71 us
    unnamed x8, local copies, waits for them, and re-layouts  2.93 us
  transfers between devices with their start and end apart: 6, of which 2 were waited for; matrix products, arithmetic and copies ran while one was open for 0% of the time, Pallas kernels for 8%

profile of v2, /device:TPU:8, one launch (start us, length us, event | category | flops | bytes accessed | tf_op | source)
XLA Modules:
  0.0 82.8 jit_solution(10698158750724810820)
XLA Ops:
  0.6 0.7 collective-permute-start
  1.4 5.6 %collective-permute-start.1 = (bf16[2,2,64,2048]{3,2,1,0:T(8,128)(2,1)}, bf16[2,2,64,2048]{3,2,1,0:T(8,128)(2,1)S(1)}, u32[]{:S(2)}, u32[]{:S(2)}) collective-permute-start(bf16[2,2,64,2048]{3,2,1,0:T(8,128)(2,1)} %x_ref.1), channel_id=1, source_target_pairs={{0,32},{32,0},{64,96},{96,64},{128,160},{160,128},{192,224},{224,1... | collective-permute-start | bytes 3145736 | tf_op jit(solution)/shard_map/ppermute | solution.py:269
  7.0 0.0 copy-start.2
  7.0 0.0 copy-start.3
  7.0 0.7 copy-done.2
  7.6 0.0 copy-done.3
  7.7 0.0 copy-start.1
  7.7 1.0 %copy-done.1 = bf16[2,64,2048]{2,1,0:T(8,128)(2,1)S(1)} copy-done((bf16[2,64,2048]{2,1,0:T(8,128)(2,1)S(1)}, bf16[2,64,2048]{2,1,0:T(8,128)(2,1)}, u32[]{:S(2)}) %copy-start.1) | copy-done | bytes 524312
  8.7 0.7 prepare.1
  9.4 3.4 %collective-permute-start.3 = (bf16[17,64,128]{2,1,0:T(8,128)(2,1)S(1)}, bf16[17,64,128]{2,1,0:T(8,128)(2,1)S(1)}, u32[]{:S(2)}, u32[]{:S(2)}) collective-permute-start(bf16[17,64,128]{2,1,0:T(8,128)(2,1)S(1)} %get-tuple-element.9.after_ref.q0_ref), channel_id=1, source_target_pairs={{0,1},{1,0},{2,3},{3,2},{4,5},{5,4},{6,7},{7,6},{8,9},{9,8},{10,11... | collective-permute-start | bytes 835592 | tf_op jit(solution)/shard_map/ppermute | solution.py:285
  12.9 3.9 %collective-permute-start.2 = (bf16[17,64,128]{2,1,0:T(8,128)(2,1)S(1)}, bf16[17,64,128]{2,1,0:T(8,128)(2,1)S(1)}, u32[]{:S(2)}, u32[]{:S(2)}) collective-permute-start(bf16[17,64,128]{2,1,0:T(8,128)(2,1)S(1)} %get-tuple-element.10.q1_ref), channel_id=1, source_target_pairs={{0,31},{1,2},{2,1},{3,4},{4,3},{5,6},{6,5},{7,8},{8,7},{9,10},{10,... | collective-permute-start | bytes 835592 | tf_op jit(solution)/shard_map/ppermute | solution.py:285
  16.8 0.0 copy-start
  16.8 1.2 %copy-done = bf16[2,2,64,2048]{3,2,1,0:T(8,128)(2,1)S(1)} copy-done((bf16[2,2,64,2048]{3,2,1,0:T(8,128)(2,1)S(1)}, bf16[2,2,64,2048]{3,2,1,0:T(8,128)(2,1)}, u32[]{:S(2)}) %copy-start) | copy-done | bytes 1048600
  18.0 0.1 hold.1.own_ref
  18.1 1.9 %collective-permute-done.3.q_ref = bf16[17,64,128]{2,1,0:T(8,128)(2,1)S(1)} collective-permute-done((bf16[17,64,128]{2,1,0:T(8,128)(2,1)S(1)}, bf16[17,64,128]{2,1,0:T(8,128)(2,1)S(1)}, u32[]{:S(2)}, u32[]{:S(2)}) %collective-permute-start.3) | collective-permute-done | bytes 278560 | tf_op jit(solution)/shard_map/ppermute | solution.py:285
  19.9 0.0 collective-permute-done.far_ref
  19.9 0.0 collective-permute-done.1.near_ref
  19.9 1.9 %remote0.1 = bf16[17,64,128]{2,1,0:T(8,128)(2,1)S(1)} custom-call(s32[1]{0:T(128)} %bitcast.1.lat_ref, s32[1]{0:T(128)} %bitcast.lon_ref, bf16[17,64,128]{2,1,0:T(8,128)(2,1)S(1)} %collective-permute-done.3.q_ref, bf16[2,2,64,2048]{3,2,1,0:T(8,128)(2,1)S(1)} %collective-permute-done.far_ref, bf16[2,2,64,2048]{3,2,1,0:T(8,128)(2,1)S(1)} %hold.1.own_ref, ...), custom_call_target="tpu_custom_call" | custom-call | flops 268435456 | bytes 4194304 | tf_op jit(solution)/shard_map/remote0/pallas_call | solution.py:288
  21.8 3.4 %collective-permute-start.4 = (bf16[17,64,128]{2,1,0:T(8,128)(2,1)S(1)}, bf16[17,64,128]{2,1,0:T(8,128)(2,1)S(1)}, u32[]{:S(2)}, u32[]{:S(2)}) collective-permute-start(bf16[17,64,128]{2,1,0:T(8,128)(2,1)S(1)} %remote0.1), channel_id=1, source_target_pairs={{0,1},{1,0},{2,3},{3,2},{4,5},{5,4},{6,7},{7,6},{8,9},{9,8},{10,11... | collective-permute-start | bytes 835592 | tf_op jit(solution)/shard_map/ppermute | solution.py:298
  25.2 0.0 collective-permute-done.2.q_ref
  25.2 1.9 %remote1.1.after_ref = bf16[17,64,128]{2,1,0:T(8,128)(2,1)S(1)} custom-call(s32[1]{0:T(128)} %bitcast.1.lat_ref, s32[1]{0:T(128)} %bitcast.lon_ref, bf16[17,64,128]{2,1,0:T(8,128)(2,1)S(1)} %collective-permute-done.2.q_ref, bf16[2,2,64,2048]{3,2,1,0:T(8,128)(2,1)S(1)} %collective-permute-done.far_ref, bf16[2,2,64,2048]{3,2,1,0:T(8,128)(2,1)S(1)} %hold.1.own_ref, ...), custom_call_target="tpu_custom_call" | custom-call | flops 268435456 | bytes 4194304 | tf_op jit(solution)/shard_map/remote1/pallas_call | solution.py:288
  27.0 5.0 %collective-permute-start.5 = (bf16[17,64,128]{2,1,0:T(8,128)(2,1)S(1)}, bf16[17,64,128]{2,1,0:T(8,128)(2,1)S(1)}, u32[]{:S(2)}, u32[]{:S(2)}) collective-permute-start(bf16[17,64,128]{2,1,0:T(8,128)(2,1)S(1)} %remote1.1.after_ref), channel_id=1, source_target_pairs={{0,31},{1,2},{2,1},{3,4},{4,3},{5,6},{6,5},{7,8},{8,7},{9,10},{10,... | collective-permute-start | bytes 835592 | tf_op jit(solution)/shard_map/ppermute | solution.py:298
  32.0 1.9 %own.1 = (bf16[16,128,128]{2,1,0:T(8,128)(2,1)S(1)}, f32[128,128]{1,0:T(8,128)S(1)}, f32[128,128]{1,0:T(8,128)S(1)}) custom-call(s32[1]{0:T(128)} %bitcast.1.lat_ref, s32[1]{0:T(128)} %bitcast.lon_ref, bf16[17,64,128]{2,1,0:T(8,128)(2,1)S(1)} %get-tuple-element.9.after_ref.q0_ref, bf16[17,64,128]{2,1,0:T(8,128)(2,1)S(1)} %get-tuple-element.10.q1_ref, ...), custom_call_target="tpu_custom_call" | custom-call | flops 536870912 | bytes 4194304 | tf_op jit(solution)/shard_map/own/pallas_call | solution.py:299
  34.0 0.0 collective-permute-done.4.part0_ref
  34.0 4.5 %collective-permute-done.5.part1_ref = bf16[17,64,128]{2,1,0:T(8,128)(2,1)S(1)} collective-permute-done((bf16[17,64,128]{2,1,0:T(8,128)(2,1)S(1)}, bf16[17,64,128]{2,1,0:T(8,128)(2,1)S(1)}, u32[]{:S(2)}, u32[]{:S(2)}) %collective-permute-start.5) | collective-permute-done | bytes 278560 | tf_op jit(solution)/shard_map/ppermute | solution.py:298
  38.5 2.4 %combine.1 = (bf16[2,64,2048]{2,1,0:T(8,128)(2,1)}, bf16[32,40,128]{2,1,0:T(8,128)(2,1)S(1)}) custom-call(s32[1]{0:T(128)} %bitcast.lon_ref, bf16[16,128,128]{2,1,0:T(8,128)(2,1)S(1)} %get-tuple-element.11.own_ref, f32[128,128]{1,0:T(8,128)S(1)} %get-tuple-element.12.top_ref, f32[128,128]{1,0:T(8,128)S(1)} %get-tuple-element.13.total_ref, ...), custom_call_target="tpu_custom_call" | custom-call | tf_op jit(solution)/shard_map/combine/pallas_call | solution.py:307
  40.9 23.7 %all_to_all.10.x_ref = bf16[32,40,128]{2,1,0:T(8,128)(2,1)S(1)} all-to-all(bf16[32,40,128]{2,1,0:T(8,128)(2,1)S(1)} %get-tuple-element.15), channel_id=1, replica_groups=mesh['lat'=24,'lon'=32] {'lon'}, dimensions={0} | all-to-all | bytes 655360 | tf_op jit(solution)/shard_map/all_to_all | solution.py:313
  64.6 0.1 total.1
  64.7 16.8 %all_to_all.11.x_ref = bf16[32,40,128]{2,1,0:T(8,128)(2,1)S(1)} all-to-all(bf16[32,40,128]{2,1,0:T(8,128)(2,1)S(1)} %total.1), channel_id=1, replica_groups=mesh['lat'=24,'lon'=32] {'lon'}, dimensions={0} | all-to-all | bytes 655360 | tf_op jit(solution)/shard_map/all_to_all | solution.py:315
  81.5 1.4 %unpack.1 = f32[1,16,128,128]{3,2,1,0:T(8,128)} custom-call(bf16[32,40,128]{2,1,0:T(8,128)(2,1)S(1)} %all_to_all.11.x_ref), custom_call_target="tpu_custom_call" | custom-call | tf_op jit(solution)/shard_map/unpack/pallas_call | solution.py:316
Async XLA Ops:
  0.6 19.3 %collective-permute-start = (bf16[2,2,64,2048]{3,2,1,0:T(8,128)(2,1)}, bf16[2,2,64,2048]{3,2,1,0:T(8,128)(2,1)S(1)}, u32[]{:S(2)}, u32[]{:S(2)}) collective-permute-start(bf16[2,2,64,2048]{3,2,1,0:T(8,128)(2,1)} %x_ref.1), channel_id=1, source_target_pairs={{32,64},{64,32},{96,128},{128,96},{160,192},{192,160},{224,256},{2... | collective-permute-start | bytes 3145736 | tf_op jit(solution)/shard_map/ppermute | solution.py:268
  1.4 18.6 %collective-permute-start.1 = (bf16[2,2,64,2048]{3,2,1,0:T(8,128)(2,1)}, bf16[2,2,64,2048]{3,2,1,0:T(8,128)(2,1)S(1)}, u32[]{:S(2)}, u32[]{:S(2)}) collective-permute-start(bf16[2,2,64,2048]{3,2,1,0:T(8,128)(2,1)} %x_ref.1), channel_id=1, source_target_pairs={{0,32},{32,0},{64,96},{96,64},{128,160},{160,128},{192,224},{224,1... | collective-permute-start | bytes 3145736 | tf_op jit(solution)/shard_map/ppermute | solution.py:269
  7.0 0.7 copy-start.2
  7.0 0.7 copy-start.3
  7.7 1.0 %copy-start.1 = (bf16[2,64,2048]{2,1,0:T(8,128)(2,1)S(1)}, bf16[2,64,2048]{2,1,0:T(8,128)(2,1)}, u32[]{:S(2)}) copy-start(bf16[2,64,2048]{2,1,0:T(8,128)(2,1)} %q_hbm.1) | copy-start | bytes 1572868
  9.4 10.5 %collective-permute-start.3 = (bf16[17,64,128]{2,1,0:T(8,128)(2,1)S(1)}, bf16[17,64,128]{2,1,0:T(8,128)(2,1)S(1)}, u32[]{:S(2)}, u32[]{:S(2)}) collective-permute-start(bf16[17,64,128]{2,1,0:T(8,128)(2,1)S(1)} %get-tuple-element.9.after_ref.q0_ref), channel_id=1, source_target_pairs={{0,1},{1,0},{2,3},{3,2},{4,5},{5,4},{6,7},{7,6},{8,9},{9,8},{10,11... | collective-permute-start | bytes 835592 | tf_op jit(solution)/shard_map/ppermute | solution.py:285
  12.9 12.3 %collective-permute-start.2 = (bf16[17,64,128]{2,1,0:T(8,128)(2,1)S(1)}, bf16[17,64,128]{2,1,0:T(8,128)(2,1)S(1)}, u32[]{:S(2)}, u32[]{:S(2)}) collective-permute-start(bf16[17,64,128]{2,1,0:T(8,128)(2,1)S(1)} %get-tuple-element.10.q1_ref), channel_id=1, source_target_pairs={{0,31},{1,2},{2,1},{3,4},{4,3},{5,6},{6,5},{7,8},{8,7},{9,10},{10,... | collective-permute-start | bytes 835592 | tf_op jit(solution)/shard_map/ppermute | solution.py:285
  16.8 1.2 %copy-start = (bf16[2,2,64,2048]{3,2,1,0:T(8,128)(2,1)S(1)}, bf16[2,2,64,2048]{3,2,1,0:T(8,128)(2,1)}, u32[]{:S(2)}) copy-start(bf16[2,2,64,2048]{3,2,1,0:T(8,128)(2,1)} %x_ref.1) | copy-start | bytes 3145732
  21.8 12.2 %collective-permute-start.4 = (bf16[17,64,128]{2,1,0:T(8,128)(2,1)S(1)}, bf16[17,64,128]{2,1,0:T(8,128)(2,1)S(1)}, u32[]{:S(2)}, u32[]{:S(2)}) collective-permute-start(bf16[17,64,128]{2,1,0:T(8,128)(2,1)S(1)} %remote0.1), channel_id=1, source_target_pairs={{0,1},{1,0},{2,3},{3,2},{4,5},{5,4},{6,7},{7,6},{8,9},{9,8},{10,11... | collective-permute-start | bytes 835592 | tf_op jit(solution)/shard_map/ppermute | solution.py:298
  27.0 11.5 %collective-permute-start.5 = (bf16[17,64,128]{2,1,0:T(8,128)(2,1)S(1)}, bf16[17,64,128]{2,1,0:T(8,128)(2,1)S(1)}, u32[]{:S(2)}, u32[]{:S(2)}) collective-permute-start(bf16[17,64,128]{2,1,0:T(8,128)(2,1)S(1)} %remote1.1.after_ref), channel_id=1, source_target_pairs={{0,31},{1,2},{2,1},{3,4},{4,3},{5,6},{6,5},{7,8},{8,7},{9,10},{10,... | collective-permute-start | bytes 835592 | tf_op jit(solution)/shard_map/ppermute | solution.py:298

commit v3 on v2

--- a/solution.py
+++ b/solution.py
@@ -13,8 +13,10 @@
 HALO = 2
 CAND = 15
 NB = 13
-ROWS = 40
+ROWS = 32
 NEG = -1e30
+COPIED = 4
+OWN_GROUP, REMOTE_GROUP, COMBINE_GROUP = 1, 8, 8
 LOG2 = 1.4426950408889634 * HD ** (-0.5)
 
 VMEM = pl.BlockSpec(memory_space=pltpu.VMEM)
@@ -43,7 +45,7 @@
     lane = iota((1, 128), 1)
     copies[0].wait()
     copies[1].wait()
-    for b, out in ((1 - odd, out0_ref), (odd, out1_ref)):
+    for b, out in ((odd, out0_ref), (1 - odd, out1_ref)):
         for t in range(2):
             listed = jnp.zeros((1, 128), jnp.int32)
             for n in range(NB):
@@ -61,7 +63,7 @@
             seen = jnp.broadcast_to(seen, (BLOCK, 128)).astype(jnp.bfloat16)
             out[HEADS, t * BLOCK : (t + 1) * BLOCK, :] = seen
     copies[2].wait()
-    for b, out in ((1 - odd, out0_ref), (odd, out1_ref)):
+    for b, out in ((odd, out0_ref), (1 - odd, out1_ref)):
         cells = pl.ds(pl.multiple_of(b * BLOCK, BLOCK), BLOCK)
         for t in range(2):
             for h in range(HEADS):
@@ -95,13 +97,14 @@
     return lax.dot_general(q, keys, (((1,), (1,)), ((), ())), preferred_element_type=jnp.float32)
 
 
-def staged(*stages):
+def staged(group, *stages):
     held = [{} for _ in stages]
-    for step in range(HEADS + len(stages) - 1):
+    groups = HEADS // group
+    for step in range(groups + len(stages) - 1):
         for i, stage in enumerate(stages):
-            h = step - i
-            if 0 <= h < HEADS:
-                held[i][h] = stage(h) if i == 0 else stage(h, held[i - 1].pop(h))
+            if 0 <= step - i < groups:
+                for h in range((step - i) * group, (step - i + 1) * group):
+                    held[i][h] = stage(h) if i == 0 else stage(h, held[i - 1].pop(h))
 
 
 def softmax_stage(bias, stats):
@@ -114,7 +117,7 @@
         total = jnp.sum(weights, axis=-1, keepdims=True)
         stats[0] = jnp.where(lane == h, top, stats[0])
         stats[1] = jnp.where(lane == h, total, stats[1])
-        return weights.astype(jnp.bfloat16)
+        return weights.astype(jnp.bfloat16), 1.0 / total
 
     return stage
 
@@ -127,7 +130,7 @@
     bias = jnp.concatenate(
         [
             bias_of(ref[HEADS, t * BLOCK : (t + 1) * BLOCK, :], t, lat_odd, 2, -b)
-            for b, ref in ((1 - odd, q0_ref), (odd, q1_ref))
+            for b, ref in ((odd, q0_ref), (1 - odd, q1_ref))
             for t in range(2)
         ],
         axis=0,
@@ -137,11 +140,12 @@
     def score(h):
         return scores_of(jnp.concatenate([q0_ref[h], q1_ref[h]], axis=0), rows_of(refs, 0, cells, h))
 
-    def mix(h, weights):
+    def mix(h, softmax):
+        weights, inverse = softmax
         mixed = jnp.dot(weights, rows_of(refs, 1, cells, h), preferred_element_type=jnp.float32)
-        out_ref[h] = mixed.astype(jnp.bfloat16)
-
-    staged(score, softmax_stage(bias, stats), mix)
+        out_ref[h] = (mixed * inverse).astype(jnp.bfloat16)
+
+    staged(OWN_GROUP, score, softmax_stage(bias, stats), mix)
     top_ref[...] = stats[0]
     total_ref[...] = stats[1]
 
@@ -156,7 +160,7 @@
 def remote_body(partner, lat_ref, lon_ref, q_ref, far_ref, own_ref, near_ref, out_ref):
     refs = (far_ref, own_ref, near_ref)
     lat_odd, odd = place(lat_ref, lon_ref)
-    held = 1 - odd if partner == 0 else odd
+    held = odd if partner == 0 else 1 - odd
     cells = pl.ds(pl.multiple_of(held * BLOCK, BLOCK), BLOCK)
     bias = jnp.concatenate(
         [
@@ -170,11 +174,12 @@
     def score(h):
         return scores_of(q_ref[h], rows_of(refs, 0, cells, h))
 
-    def mix(h, weights):
+    def mix(h, softmax):
+        weights, inverse = softmax
         mixed = jnp.dot(weights, rows_of(refs, 1, cells, h), preferred_element_type=jnp.float32)
-        out_ref[h] = mixed.astype(jnp.bfloat16)
-
-    staged(score, softmax_stage(bias, stats), mix)
+        out_ref[h] = (mixed * inverse).astype(jnp.bfloat16)
+
+    staged(REMOTE_GROUP, score, softmax_stage(bias, stats), mix)
     lane = iota((2 * BLOCK, 128), 1)
     packed = jnp.zeros((2 * BLOCK, 128), jnp.float32)
     for i, part in enumerate(thirds(stats[0]) + thirds(stats[1])):
@@ -183,7 +188,7 @@
     out_ref[HEADS] = packed.astype(jnp.bfloat16)
 
 
-def combine_body(lon_ref, own_ref, top_ref, total_ref, part0_ref, part1_ref, out_ref, packed_ref):
+def combine_body(lon_ref, own_ref, top_ref, total_ref, part0_ref, part1_ref, out_hbm, packed_ref, diag_ref, out_ref, sems):
     half = 2 * BLOCK
     odd = lax.rem(lon_ref[0], 2)
     split = jnp.concatenate([part0_ref[HEADS], part1_ref[HEADS]], axis=0).astype(jnp.float32)
@@ -195,20 +200,31 @@
     far_total = jnp.where(lane < HEADS, far_total, 1.0)
     near_top = top_ref[...]
     top = jnp.maximum(near_top, far_top)
-    mine, theirs = jnp.exp2(near_top - top), jnp.exp2(far_top - top)
-    inverse = 1.0 / (mine * total_ref[...] + theirs * far_total)
-    mine, theirs = mine * inverse, theirs * inverse
+    mine = jnp.exp2(near_top - top) * total_ref[...]
+    theirs = jnp.exp2(far_top - top) * far_total
+    share = theirs / (mine + theirs)
     row, lane = iota((64, 128), 0), iota((64, 128), 1)
+    pair, side = iota((8, 128), 0), iota((8, 128), 1)
+    diagonals = [jnp.zeros((8, 128), jnp.float32)]
+    copies = []
 
     def merge(h):
         far = jnp.concatenate([part0_ref[h], part1_ref[h]], axis=0).astype(jnp.float32)
         near = own_ref[h].astype(jnp.float32)
-        cells = (near * mine[:, h : h + 1] + far * theirs[:, h : h + 1]).astype(jnp.bfloat16)
-        for i, b in enumerate((1 - odd, odd)):
+        cells = (near + (far - near) * share[:, h : h + 1]).astype(jnp.bfloat16)
+        for i, b in enumerate((odd, 1 - odd)):
             place_b = pl.ds(pl.multiple_of(b * BLOCK, BLOCK), BLOCK)
             for t in range(2):
                 low = i * half + t * BLOCK
                 out_ref[t, place_b, h * HD : (h + 1) * HD] = cells[low : low + BLOCK]
+        if h % COPIED == COPIED - 1:
+            features = slice((h + 1 - COPIED) * HD, (h + 1) * HD)
+            copies.append(
+                pltpu.make_async_copy(
+                    out_ref.at[:, :, features], out_hbm.at[:, :, features], sems.at[h // COPIED]
+                )
+            )
+            copies[-1].start()
         return cells
 
     def multiply(h, cells):
@@ -218,37 +234,52 @@
         upper, lower = gram[:64], gram[64:]
         folded = jnp.where((lane < 64) & (row > lane), pltpu.roll(lower, 64, 1), upper).astype(jnp.bfloat16)
         diagonal = jnp.sum(jnp.where(lane - 64 == row, lower, 0.0), axis=0, keepdims=True)
-        diagonal = jnp.broadcast_to(diagonal, (8, 128)).astype(jnp.bfloat16)
+        if h % 2 == 0:
+            diagonal = pltpu.roll(diagonal, 64, 1)
+        mine_here = (pair == h // 2) & (side // 64 == h % 2)
+        diagonals[0] = jnp.where(mine_here, diagonal, diagonals[0])
         for part in range(2):
-            packed_ref[2 * h + part, :32, :] = folded[part * 32 : (part + 1) * 32]
-            packed_ref[2 * h + part, 32:, :] = diagonal
-
-    staged(merge, multiply, pack)
-
-
-def sum_body(x_ref, out_ref):
+            packed_ref[2 * h + part] = folded[part * 32 : (part + 1) * 32]
+
+    staged(COMBINE_GROUP, merge, multiply, pack)
+    diag_ref[...] = diagonals[0].astype(jnp.bfloat16)
+    for copy in copies:
+        copy.wait()
+
+
+def sum_body(x_ref, diag_ref, out_ref):
     total = jnp.sum(x_ref[...].astype(jnp.float32), axis=0).astype(jnp.bfloat16)
-    out_ref[...] = jnp.broadcast_to(total[None], out_ref.shape)
-
-
-def unpack_body(x_ref, out_ref):
+    out_ref[:, :ROWS, :] = jnp.broadcast_to(total[None], (2 * HEADS, ROWS, 128))
+    out_ref[:, ROWS:, :] = jnp.broadcast_to(diag_ref[...][None], (2 * HEADS, 8, 128))
+
+
+def unpack_body(x_ref, out_hbm, out_ref, sems):
     row, lane = iota((64, 128), 0), iota((64, 128), 1)
+    odd_diagonals = jnp.sum(x_ref[:, ROWS:, :].astype(jnp.float32), axis=0)
+    even_diagonals = pltpu.roll(odd_diagonals, 64, 1)
+    copies = []
     for h in range(HEADS):
-        folded = jnp.concatenate([x_ref[2 * h, :32, :], x_ref[2 * h + 1, :32, :]], axis=0).astype(jnp.float32)
-        diagonal = x_ref[2 * h, 32:, :].astype(jnp.float32)[:1]
+        folded = jnp.concatenate([x_ref[2 * h, :ROWS, :], x_ref[2 * h + 1, :ROWS, :]], axis=0).astype(jnp.float32)
+        diagonal = (odd_diagonals if h % 2 else even_diagonals)[h // 2 : h // 2 + 1]
         turned = jnp.concatenate([folded, jnp.zeros_like(folded)], axis=0).T
         out_ref[0, h, :64, :] = jnp.where((lane < 64) & (row > lane), turned[:64], folded)
         corner = pltpu.roll(jnp.where(row > lane, folded, turned[:64]), 64, 1)
         corner = jnp.where(lane - 64 == row, diagonal, corner)
         out_ref[0, h, 64:, :] = jnp.where(lane < 64, turned[64:], corner)
-
-
-def call(body, outs, specs, flops=0, moved=0, name=None, scratch=()):
+        if h % 2:
+            pair = pl.ds(h - 1, 2)
+            copies.append(pltpu.make_async_copy(out_ref.at[:, pair], out_hbm.at[:, pair], sems.at[h // 2]))
+            copies[-1].start()
+    for copy in copies:
+        copy.wait()
+
+
+def call(body, outs, specs, flops=0, moved=0, name=None, scratch=(), places=None):
     return pl.pallas_call(
         body,
         out_shape=[jax.ShapeDtypeStruct(shape, dtype) for shape, dtype in outs],
         in_specs=specs,
-        out_specs=[VMEM] * len(outs),
+        out_specs=places or [VMEM] * len(outs),
         scratch_shapes=scratch,
         compiler_params=pltpu.CompilerParams(vmem_limit_bytes=40 << 20),
         cost_estimate=pl.CostEstimate(flops=flops, bytes_accessed=moved, transcendentals=0),
@@ -261,7 +292,7 @@
     lats, lons = lax.axis_size("lat"), lax.axis_size("lon")
     chips = [(i, i + 1 if i % 2 else i - 1) for i in range(1, lats - 1)]
     cores = [(i, i ^ 1) for i in range(lats)]
-    pairs = [(i, i ^ 1) for i in range(lons)], [(i, (i + (1 if i % 2 else -1)) % lons) for i in range(lons)]
+    pairs = [(i, (i + (1 if i % 2 else -1)) % lons) for i in range(lons)], [(i, i ^ 1) for i in range(lons)]
     edge = ((HEADS + 1, 2 * BLOCK, HD), bf16)
     level = ((4 * BLOCK, 128), f32)
 
@@ -281,7 +312,7 @@
             pltpu.VMEM(queries.shape, bf16),
             pltpu.SemaphoreType.DMA((3,)),
         ],
-    )(lat, lon, keep, lists, queries)
+    )(lat, lon, *[pltpu.with_memory_space_constraint(x, pltpu.HBM) for x in (keep, lists, queries)])
     theirs = [lax.ppermute(x, "lon", pair) for x, pair in zip(mine, pairs)]
     (held,) = call(hold_body, [(keyval.shape, bf16)], [VMEM, ANY], moved=2 << 20, name="hold")(keyval, mine[0])
     answers = [
@@ -304,16 +335,26 @@
         moved=4 << 20,
         name="own",
     )(lat, lon, *mine, far, held, near, answers[1])
-    attended, packed = call(
+    attended, packed, diagonals = call(
         combine_body,
-        [(queries.shape, bf16), ((2 * HEADS, ROWS, 128), bf16)],
+        [(queries.shape, bf16), ((2 * HEADS, ROWS, 128), bf16), ((8, 128), bf16)],
         [SMEM] + [VMEM] * 5,
         name="combine",
+        scratch=[pltpu.VMEM(queries.shape, bf16), pltpu.SemaphoreType.DMA((HEADS // COPIED,))],
+        places=[HBM, VMEM, VMEM],
     )(lon, own, top, total, *parts)
     swapped = lax.all_to_all(packed, "lon", 0, 0, tiled=True)
-    (summed,) = call(sum_body, [((2 * HEADS, ROWS, 128), bf16)], [VMEM], name="total")(swapped)
+    (summed,) = call(sum_body, [((2 * HEADS, ROWS + 8, 128), bf16)], [VMEM] * 2, name="total")(swapped, diagonals)
     gathered = lax.all_to_all(summed, "lon", 0, 0, tiled=True)
-    (gram,) = call(unpack_body, [((1, HEADS, HD, HD), f32)], [VMEM], name="unpack")(gathered)
+    gram_shape = (1, HEADS, HD, HD)
+    (gram,) = call(
+        unpack_body,
+        [(gram_shape, f32)],
+        [VMEM],
+        name="unpack",
+        scratch=[pltpu.VMEM(gram_shape, f32), pltpu.SemaphoreType.DMA((HEADS // 2,))],
+        places=[HBM],
+    )(gathered)
     return attended, gram
 
 

time: 83.3 us -> 78.3 us (0.940)
  waiting for transfers between devices: 6.38 us -> 9.92 us
  starting transfers between devices: 22 us -> 19.6 us
  Pallas kernels: 10.3 us -> 7.92 us
  blocking collectives: 40.5 us -> 38.5 us
  local copies, waits for them, and re-layouts: 2.93 us -> 1.22 us
    ppermute x2, waiting for transfers between devices: 1.87 us -> 4.47 us  [local(): theirs = [lax.ppermute(x, 'lon', pair) for x, pair in zip(mine, pairs)]]
    ppermute x2, starting transfers between devices: 8.39 us -> 6.46 us  [local(): parts = [lax.ppermute(x, 'lon', pair) for x, pair in zip(answers, pairs)]]
    unnamed x8 -> x2, local copies, waits for them, and re-layouts: 2.93 us -> 1.22 us
    pallas_call x2, Pallas kernels: 3.71 us -> 2.1 us  [local(): call(functools.partial(remote_body, i), [edge], [SMEM, SMEM] + [VMEM] * 4...]
    all_to_all x1, blocking collectives: 16.8 us -> 15.6 us  [local(): gathered = lax.all_to_all(summed, 'lon', 0, 0, tiled=True)]
    pallas_call x1, Pallas kernels: 2.39 us -> 1.31 us  [local(): call(combine_body, [(queries.shape, bf16), ((2 * HEADS, ROWS, 128), bf16)...]
    ppermute x2, waiting for transfers between devices: 4.51 us -> 5.45 us  [local(): parts = [lax.ppermute(x, 'lon', pair) for x, pair in zip(answers, pairs)]]
  transfers between devices with their start and end apart: 6 -> 6, of which waited for: 2 -> 3; matrix products, arithmetic and copies ran while one was open for 0% -> 0% of each run, Pallas kernels for 8% -> 7%
where the time goes in v3:
time: 78.3 us; the launch traced here: 77.9 us
  blocking collectives  38.5 us (49%)
  starting transfers between devices  19.6 us (25%)
  waiting for transfers between devices  9.92 us (13%)
  Pallas kernels  7.92 us (10%)
  local copies, waits for them, and re-layouts  1.22 us (2%)
    all_to_all x1, blocking collectives, local(): swapped = lax.all_to_all(packed, 'lon', 0, 0, tiled=True)  22.9 us
    all_to_all x1, blocking collectives, local(): gathered = lax.all_to_all(summed, 'lon', 0, 0, tiled=True)  15.6 us
    ppermute x2, starting transfers between devices, local(): theirs = [lax.ppermute(x, 'lon', pair) for x, pair in zip(mine, pairs)]  6.8 us
    ppermute x2, starting transfers between devices, local(): parts = [lax.ppermute(x, 'lon', pair) for x, pair in zip(answers, pairs)]  6.46 us
    ppermute x1, starting transfers between devices, local(): near = lax.ppermute(keyval, 'lat', cores)  5.58 us
    ppermute x2, waiting for transfers between devices, local(): parts = [lax.ppermute(x, 'lon', pair) for x, pair in zip(answers, pairs)]  5.45 us
    ppermute x2, waiting for transfers between devices, local(): theirs = [lax.ppermute(x, 'lon', pair) for x, pair in zip(mine, pairs)]  4.47 us
    pallas_call x2, Pallas kernels, local(): call(functools.partial(remote_body, i), [edge], [SMEM, SMEM] + [VMEM] * 4...  2.1 us
  transfers between devices with their start and end apart: 6, of which 3 were waited for; matrix products, arithmetic and copies ran while one was open for 0% of the time, Pallas kernels for 7%

profile of v3, /device:TPU:8, one launch (start us, length us, event | category | flops | bytes accessed | tf_op | source)
XLA Modules:
  0.0 77.9 jit_solution(11309710708097362996)
XLA Ops:
  0.6 0.7 collective-permute-start
  1.4 5.6 %collective-permute-start.1 = (bf16[2,2,64,2048]{3,2,1,0:T(8,128)(2,1)}, bf16[2,2,64,2048]{3,2,1,0:T(8,128)(2,1)S(1)}, u32[]{:S(2)}, u32[]{:S(2)}) collective-permute-start(bf16[2,2,64,2048]{3,2,1,0:T(8,128)(2,1)} %x_ref.1), channel_id=1, source_target_pairs={{0,32},{32,0},{64,96},{96,64},{128,160},{160,128},{192,224},{224,1... | collective-permute-start | bytes 3145736 | tf_op jit(solution)/shard_map/ppermute | solution.py:300
  7.0 1.2 %prepare.1 = (bf16[17,64,128]{2,1,0:T(8,128)(2,1)S(1)}, bf16[17,64,128]{2,1,0:T(8,128)(2,1)S(1)}) custom-call(s32[1]{0:T(128)} %bitcast.1.lat_ref, s32[1]{0:T(128)} %bitcast.lon_ref, s32[48]{0:T(128)} %keep_hbm.1, s32[2,2,13]{2,1,0:T(2,128)} %lists_hbm.1, bf16[2,64,2048]{2,1,0:T(8,128)(2,1)} %q_hbm.1), custom_call_target="tpu_custom_call" | custom-call | bytes 1048576 | tf_op jit(solution)/shard_map/prepare/pallas_call | solution.py:303
  8.1 4.6 %collective-permute-start.3 = (bf16[17,64,128]{2,1,0:T(8,128)(2,1)S(1)}, bf16[17,64,128]{2,1,0:T(8,128)(2,1)S(1)}, u32[]{:S(2)}, u32[]{:S(2)}) collective-permute-start(bf16[17,64,128]{2,1,0:T(8,128)(2,1)S(1)} %get-tuple-element.10.after_ref.q0_ref), channel_id=1, source_target_pairs={{0,31},{1,2},{2,1},{3,4},{4,3},{5,6},{6,5},{7,8},{8,7},{9,10},{10,... | collective-permute-start | bytes 835592 | tf_op jit(solution)/shard_map/ppermute | solution.py:316
  12.7 2.2 %collective-permute-start.2 = (bf16[17,64,128]{2,1,0:T(8,128)(2,1)S(1)}, bf16[17,64,128]{2,1,0:T(8,128)(2,1)S(1)}, u32[]{:S(2)}, u32[]{:S(2)}) collective-permute-start(bf16[17,64,128]{2,1,0:T(8,128)(2,1)S(1)} %get-tuple-element.11.q1_ref), channel_id=1, source_target_pairs={{0,1},{1,0},{2,3},{3,2},{4,5},{5,4},{6,7},{7,6},{8,9},{9,8},{10,11... | collective-permute-start | bytes 835592 | tf_op jit(solution)/shard_map/ppermute | solution.py:316
  14.9 0.0 copy-start
  15.0 1.2 %copy-done = bf16[2,2,64,2048]{3,2,1,0:T(8,128)(2,1)S(1)} copy-done((bf16[2,2,64,2048]{3,2,1,0:T(8,128)(2,1)S(1)}, bf16[2,2,64,2048]{3,2,1,0:T(8,128)(2,1)}, u32[]{:S(2)}) %copy-start) | copy-done | bytes 1048600
  16.2 0.1 hold.1.own_ref
  16.2 4.5 %collective-permute-done.3.q_ref = bf16[17,64,128]{2,1,0:T(8,128)(2,1)S(1)} collective-permute-done((bf16[17,64,128]{2,1,0:T(8,128)(2,1)S(1)}, bf16[17,64,128]{2,1,0:T(8,128)(2,1)S(1)}, u32[]{:S(2)}, u32[]{:S(2)}) %collective-permute-start.3) | collective-permute-done | bytes 278560 | tf_op jit(solution)/shard_map/ppermute | solution.py:316
  20.7 0.0 collective-permute-done.far_ref
  20.7 0.0 collective-permute-done.1.near_ref
  20.7 1.0 %remote0.1 = bf16[17,64,128]{2,1,0:T(8,128)(2,1)S(1)} custom-call(s32[1]{0:T(128)} %bitcast.1.lat_ref, s32[1]{0:T(128)} %bitcast.lon_ref, bf16[17,64,128]{2,1,0:T(8,128)(2,1)S(1)} %collective-permute-done.3.q_ref, bf16[2,2,64,2048]{3,2,1,0:T(8,128)(2,1)S(1)} %collective-permute-done.far_ref, bf16[2,2,64,2048]{3,2,1,0:T(8,128)(2,1)S(1)} %hold.1.own_ref, ...), custom_call_target="tpu_custom_call" | custom-call | flops 268435456 | bytes 4194304 | tf_op jit(solution)/shard_map/remote0/pallas_call | solution.py:319
  21.8 4.5 %collective-permute-start.4 = (bf16[17,64,128]{2,1,0:T(8,128)(2,1)S(1)}, bf16[17,64,128]{2,1,0:T(8,128)(2,1)S(1)}, u32[]{:S(2)}, u32[]{:S(2)}) collective-permute-start(bf16[17,64,128]{2,1,0:T(8,128)(2,1)S(1)} %remote0.1), channel_id=1, source_target_pairs={{0,31},{1,2},{2,1},{3,4},{4,3},{5,6},{6,5},{7,8},{8,7},{9,10},{10,... | collective-permute-start | bytes 835592 | tf_op jit(solution)/shard_map/ppermute | solution.py:329
  26.3 0.0 collective-permute-done.2.q_ref
  26.3 1.1 %remote1.1.after_ref = bf16[17,64,128]{2,1,0:T(8,128)(2,1)S(1)} custom-call(s32[1]{0:T(128)} %bitcast.1.lat_ref, s32[1]{0:T(128)} %bitcast.lon_ref, bf16[17,64,128]{2,1,0:T(8,128)(2,1)S(1)} %collective-permute-done.2.q_ref, bf16[2,2,64,2048]{3,2,1,0:T(8,128)(2,1)S(1)} %collective-permute-done.far_ref, bf16[2,2,64,2048]{3,2,1,0:T(8,128)(2,1)S(1)} %hold.1.own_ref, ...), custom_call_target="tpu_custom_call" | custom-call | flops 268435456 | bytes 4194304 | tf_op jit(solution)/shard_map/remote1/pallas_call | solution.py:319
  27.4 1.9 %collective-permute-start.5 = (bf16[17,64,128]{2,1,0:T(8,128)(2,1)S(1)}, bf16[17,64,128]{2,1,0:T(8,128)(2,1)S(1)}, u32[]{:S(2)}, u32[]{:S(2)}) collective-permute-start(bf16[17,64,128]{2,1,0:T(8,128)(2,1)S(1)} %remote1.1.after_ref), channel_id=1, source_target_pairs={{0,1},{1,0},{2,3},{3,2},{4,5},{5,4},{6,7},{7,6},{8,9},{9,8},{10,11... | collective-permute-start | bytes 835592 | tf_op jit(solution)/shard_map/ppermute | solution.py:329
  29.3 2.0 %own.1 = (bf16[16,128,128]{2,1,0:T(8,128)(2,1)S(1)}, f32[128,128]{1,0:T(8,128)S(1)}, f32[128,128]{1,0:T(8,128)S(1)}) custom-call(s32[1]{0:T(128)} %bitcast.1.lat_ref, s32[1]{0:T(128)} %bitcast.lon_ref, bf16[17,64,128]{2,1,0:T(8,128)(2,1)S(1)} %get-tuple-element.10.after_ref.q0_ref, bf16[17,64,128]{2,1,0:T(8,128)(2,1)S(1)} %get-tuple-element.11.q1_ref, ...), custom_call_target="tpu_custom_call" | custom-call | flops 536870912 | bytes 4194304 | tf_op jit(solution)/shard_map/own/pallas_call | solution.py:330
  31.3 2.2 %collective-permute-done.4.part0_ref = bf16[17,64,128]{2,1,0:T(8,128)(2,1)S(1)} collective-permute-done((bf16[17,64,128]{2,1,0:T(8,128)(2,1)S(1)}, bf16[17,64,128]{2,1,0:T(8,128)(2,1)S(1)}, u32[]{:S(2)}, u32[]{:S(2)}) %collective-permute-start.4) | collective-permute-done | bytes 278560 | tf_op jit(solution)/shard_map/ppermute | solution.py:329
  33.5 3.2 %collective-permute-done.5.part1_ref = bf16[17,64,128]{2,1,0:T(8,128)(2,1)S(1)} collective-permute-done((bf16[17,64,128]{2,1,0:T(8,128)(2,1)S(1)}, bf16[17,64,128]{2,1,0:T(8,128)(2,1)S(1)}, u32[]{:S(2)}, u32[]{:S(2)}) %collective-permute-start.5) | collective-permute-done | bytes 278560 | tf_op jit(solution)/shard_map/ppermute | solution.py:329
  36.7 1.3 %combine.1 = (bf16[2,64,2048]{2,1,0:T(8,128)(2,1)}, bf16[32,32,128]{2,1,0:T(8,128)(2,1)S(1)}, bf16[8,128]{1,0:T(8,128)(2,1)S(1)}) custom-call(s32[1]{0:T(128)} %bitcast.lon_ref, bf16[16,128,128]{2,1,0:T(8,128)(2,1)S(1)} %get-tuple-element.12.own_ref, f32[128,128]{1,0:T(8,128)S(1)} %get-tuple-element.13.top_ref, f32[128,128]{1,0:T(8,128)S(1)} %get-tuple-element.14.total_ref, ...), custom_call_target="tpu_custom_call" | custom-call | tf_op jit(solution)/shard_map/combine/pallas_call | solution.py:338
  38.0 22.9 %all_to_all.10.x_ref = bf16[32,32,128]{2,1,0:T(8,128)(2,1)S(1)} all-to-all(bf16[32,32,128]{2,1,0:T(8,128)(2,1)S(1)} %get-tuple-element.16), channel_id=1, replica_groups=mesh['lat'=24,'lon'=32] {'lon'}, dimensions={0} | all-to-all | bytes 524288 | tf_op jit(solution)/shard_map/all_to_all | solution.py:346
  60.9 0.1 total.1
  61.0 15.6 %all_to_all.11.x_ref = bf16[32,40,128]{2,1,0:T(8,128)(2,1)S(1)} all-to-all(bf16[32,40,128]{2,1,0:T(8,128)(2,1)S(1)} %total.1), channel_id=1, replica_groups=mesh['lat'=24,'lon'=32] {'lon'}, dimensions={0} | all-to-all | bytes 655360 | tf_op jit(solution)/shard_map/all_to_all | solution.py:348
  76.6 1.3 %unpack.1 = f32[1,16,128,128]{3,2,1,0:T(8,128)} custom-call(bf16[32,40,128]{2,1,0:T(8,128)(2,1)S(1)} %all_to_all.11.x_ref), custom_call_target="tpu_custom_call" | custom-call | tf_op jit(solution)/shard_map/unpack/pallas_call | solution.py:350
Async XLA Ops:
  0.6 20.1 %collective-permute-start = (bf16[2,2,64,2048]{3,2,1,0:T(8,128)(2,1)}, bf16[2,2,64,2048]{3,2,1,0:T(8,128)(2,1)S(1)}, u32[]{:S(2)}, u32[]{:S(2)}) collective-permute-start(bf16[2,2,64,2048]{3,2,1,0:T(8,128)(2,1)} %x_ref.1), channel_id=1, source_target_pairs={{32,64},{64,32},{96,128},{128,96},{160,192},{192,160},{224,256},{2... | collective-permute-start | bytes 3145736 | tf_op jit(solution)/shard_map/ppermute | solution.py:299
  1.4 19.4 %collective-permute-start.1 = (bf16[2,2,64,2048]{3,2,1,0:T(8,128)(2,1)}, bf16[2,2,64,2048]{3,2,1,0:T(8,128)(2,1)S(1)}, u32[]{:S(2)}, u32[]{:S(2)}) collective-permute-start(bf16[2,2,64,2048]{3,2,1,0:T(8,128)(2,1)} %x_ref.1), channel_id=1, source_target_pairs={{0,32},{32,0},{64,96},{96,64},{128,160},{160,128},{192,224},{224,1... | collective-permute-start | bytes 3145736 | tf_op jit(solution)/shard_map/ppermute | solution.py:300
  8.1 12.6 %collective-permute-start.3 = (bf16[17,64,128]{2,1,0:T(8,128)(2,1)S(1)}, bf16[17,64,128]{2,1,0:T(8,128)(2,1)S(1)}, u32[]{:S(2)}, u32[]{:S(2)}) collective-permute-start(bf16[17,64,128]{2,1,0:T(8,128)(2,1)S(1)} %get-tuple-element.10.after_ref.q0_ref), channel_id=1, source_target_pairs={{0,31},{1,2},{2,1},{3,4},{4,3},{5,6},{6,5},{7,8},{8,7},{9,10},{10,... | collective-permute-start | bytes 835592 | tf_op jit(solution)/shard_map/ppermute | solution.py:316
  12.7 13.6 %collective-permute-start.2 = (bf16[17,64,128]{2,1,0:T(8,128)(2,1)S(1)}, bf16[17,64,128]{2,1,0:T(8,128)(2,1)S(1)}, u32[]{:S(2)}, u32[]{:S(2)}) collective-permute-start(bf16[17,64,128]{2,1,0:T(8,128)(2,1)S(1)} %get-tuple-element.11.q1_ref), channel_id=1, source_target_pairs={{0,1},{1,0},{2,3},{3,2},{4,5},{5,4},{6,7},{7,6},{8,9},{9,8},{10,11... | collective-permute-start | bytes 835592 | tf_op jit(solution)/shard_map/ppermute | solution.py:316
  14.9 1.2 %copy-start = (bf16[2,2,64,2048]{3,2,1,0:T(8,128)(2,1)S(1)}, bf16[2,2,64,2048]{3,2,1,0:T(8,128)(2,1)}, u32[]{:S(2)}) copy-start(bf16[2,2,64,2048]{3,2,1,0:T(8,128)(2,1)} %x_ref.1) | copy-start | bytes 3145732
  21.8 11.7 %collective-permute-start.4 = (bf16[17,64,128]{2,1,0:T(8,128)(2,1)S(1)}, bf16[17,64,128]{2,1,0:T(8,128)(2,1)S(1)}, u32[]{:S(2)}, u32[]{:S(2)}) collective-permute-start(bf16[17,64,128]{2,1,0:T(8,128)(2,1)S(1)} %remote0.1), channel_id=1, source_target_pairs={{0,31},{1,2},{2,1},{3,4},{4,3},{5,6},{6,5},{7,8},{8,7},{9,10},{10,... | collective-permute-start | bytes 835592 | tf_op jit(solution)/shard_map/ppermute | solution.py:329
  27.4 9.3 %collective-permute-start.5 = (bf16[17,64,128]{2,1,0:T(8,128)(2,1)S(1)}, bf16[17,64,128]{2,1,0:T(8,128)(2,1)S(1)}, u32[]{:S(2)}, u32[]{:S(2)}) collective-permute-start(bf16[17,64,128]{2,1,0:T(8,128)(2,1)S(1)} %remote1.1.after_ref), channel_id=1, source_target_pairs={{0,1},{1,0},{2,3},{3,2},{4,5},{5,4},{6,7},{7,6},{8,9},{9,8},{10,11... | collective-permute-start | bytes 835592 | tf_op jit(solution)/shard_map/ppermute | solution.py:329

commit v4 on v3

--- a/solution.py
+++ b/solution.py
@@ -188,30 +188,42 @@
     out_ref[HEADS] = packed.astype(jnp.bfloat16)
 
 
-def combine_body(lon_ref, own_ref, top_ref, total_ref, part0_ref, part1_ref, out_hbm, packed_ref, diag_ref, out_ref, sems):
+def share_of(part_ref, top, total):
+    split = part_ref[HEADS].astype(jnp.float32)
+    moved = [split] + [pltpu.roll(split, 128 - i * HEADS, 1) for i in range(1, 6)]
+    lane = iota((2 * BLOCK, 128), 1)
+    far_top = jnp.where(lane < HEADS, moved[0] + moved[1] + moved[2], 0.0)
+    far_total = jnp.where(lane < HEADS, moved[3] + moved[4] + moved[5], 1.0)
+    highest = jnp.maximum(top, far_top)
+    mine = jnp.exp2(top - highest) * total
+    theirs = jnp.exp2(far_top - highest) * far_total
+    return theirs / (mine + theirs)
+
+
+def merged(near, far, share):
+    near, far = near.astype(jnp.float32), far.astype(jnp.float32)
+    return (near + (far - near) * share).astype(jnp.bfloat16)
+
+
+def merge_body(own_ref, top_ref, total_ref, part_ref, out_ref):
+    half = 2 * BLOCK
+    share = share_of(part_ref, top_ref[:half], total_ref[:half])
+    for h in range(HEADS):
+        out_ref[h] = merged(own_ref[h, :half, :], part_ref[h], share[:, h : h + 1])
+
+
+def combine_body(lon_ref, own_ref, top_ref, total_ref, first_ref, part_ref, out_hbm, packed_ref, diag_ref, out_ref, sems):
     half = 2 * BLOCK
     odd = lax.rem(lon_ref[0], 2)
-    split = jnp.concatenate([part0_ref[HEADS], part1_ref[HEADS]], axis=0).astype(jnp.float32)
-    moved = [split] + [pltpu.roll(split, 128 - i * HEADS, 1) for i in range(1, 6)]
-    far_top = moved[0] + moved[1] + moved[2]
-    far_total = moved[3] + moved[4] + moved[5]
-    lane = iota((4 * BLOCK, 128), 1)
-    far_top = jnp.where(lane < HEADS, far_top, 0.0)
-    far_total = jnp.where(lane < HEADS, far_total, 1.0)
-    near_top = top_ref[...]
-    top = jnp.maximum(near_top, far_top)
-    mine = jnp.exp2(near_top - top) * total_ref[...]
-    theirs = jnp.exp2(far_top - top) * far_total
-    share = theirs / (mine + theirs)
+    share = share_of(part_ref, top_ref[half:], total_ref[half:])
     row, lane = iota((64, 128), 0), iota((64, 128), 1)
     pair, side = iota((8, 128), 0), iota((8, 128), 1)
     diagonals = [jnp.zeros((8, 128), jnp.float32)]
     copies = []
 
     def merge(h):
-        far = jnp.concatenate([part0_ref[h], part1_ref[h]], axis=0).astype(jnp.float32)
-        near = own_ref[h].astype(jnp.float32)
-        cells = (near + (far - near) * share[:, h : h + 1]).astype(jnp.bfloat16)
+        second = merged(own_ref[h, half:, :], part_ref[h], share[:, h : h + 1])
+        cells = jnp.concatenate([first_ref[h], second], axis=0)
         for i, b in enumerate((odd, 1 - odd)):
             place_b = pl.ds(pl.multiple_of(b * BLOCK, BLOCK), BLOCK)
             for t in range(2):
@@ -335,6 +347,9 @@
         moved=4 << 20,
         name="own",
     )(lat, lon, *mine, far, held, near, answers[1])
+    (first,) = call(merge_body, [((HEADS, 2 * BLOCK, HD), bf16)], [VMEM] * 4, name="merge")(
+        own, top, total, parts[0]
+    )
     attended, packed, diagonals = call(
         combine_body,
         [(queries.shape, bf16), ((2 * HEADS, ROWS, 128), bf16), ((8, 128), bf16)],
@@ -342,7 +357,7 @@
         name="combine",
         scratch=[pltpu.VMEM(queries.shape, bf16), pltpu.SemaphoreType.DMA((HEADS // COPIED,))],
         places=[HBM, VMEM, VMEM],
-    )(lon, own, top, total, *parts)
+    )(lon, own, top, total, first, parts[1])
     swapped = lax.all_to_all(packed, "lon", 0, 0, tiled=True)
     (summed,) = call(sum_body, [((2 * HEADS, ROWS + 8, 128), bf16)], [VMEM] * 2, name="total")(swapped, diagonals)
     gathered = lax.all_to_all(summed, "lon", 0, 0, tiled=True)

time: 78.3 us -> 78.1 us (level)
  no operation moved by 1% of the time
where the time goes in v4:
time: 78.1 us; the launch traced here: 77.8 us
  blocking collectives  38.5 us (49%)
  starting transfers between devices  19.6 us (25%)
  waiting for transfers between devices  9.59 us (12%)
  Pallas kernels  8.1 us (10%)
  local copies, waits for them, and re-layouts  1.22 us (2%)
    all_to_all x1, blocking collectives, local(): swapped = lax.all_to_all(packed, 'lon', 0, 0, tiled=True)  22.9 us
    all_to_all x1, blocking collectives, local(): gathered = lax.all_to_all(summed, 'lon', 0, 0, tiled=True)  15.6 us
    ppermute x2, starting transfers between devices, local(): theirs = [lax.ppermute(x, 'lon', pair) for x, pair in zip(mine, pairs)]  6.8 us
    ppermute x2, starting transfers between devices, local(): parts = [lax.ppermute(x, 'lon', pair) for x, pair in zip(answers, pairs)]  6.46 us
    ppermute x1, starting transfers between devices, local(): near = lax.ppermute(keyval, 'lat', cores)  5.58 us
    ppermute x2, waiting for transfers between devices, local(): parts = [lax.ppermute(x, 'lon', pair) for x, pair in zip(answers, pairs)]  5.12 us
    ppermute x2, waiting for transfers between devices, local(): theirs = [lax.ppermute(x, 'lon', pair) for x, pair in zip(mine, pairs)]  4.47 us
    pallas_call x2, Pallas kernels, local(): call(functools.partial(remote_body, i), [edge], [SMEM, SMEM] + [VMEM] * 4...  2.1 us
  transfers between devices with their start and end apart: 6, of which 3 were waited for; matrix products, arithmetic and copies ran while one was open for 0% of the time, Pallas kernels for 7%

profile of v4, /device:TPU:8, one launch (start us, length us, event | category | flops | bytes accessed | tf_op | source)
XLA Modules:
  0.0 77.8 jit_solution(6080909421542955857)
XLA Ops:
  0.6 0.7 collective-permute-start
  1.4 5.6 %collective-permute-start.1 = (bf16[2,2,64,2048]{3,2,1,0:T(8,128)(2,1)}, bf16[2,2,64,2048]{3,2,1,0:T(8,128)(2,1)S(1)}, u32[]{:S(2)}, u32[]{:S(2)}) collective-permute-start(bf16[2,2,64,2048]{3,2,1,0:T(8,128)(2,1)} %x_ref.1), channel_id=1, source_target_pairs={{0,32},{32,0},{64,96},{96,64},{128,160},{160,128},{192,224},{224,1... | collective-permute-start | bytes 3145736 | tf_op jit(solution)/shard_map/ppermute | solution.py:312
  7.0 1.2 %prepare.1 = (bf16[17,64,128]{2,1,0:T(8,128)(2,1)S(1)}, bf16[17,64,128]{2,1,0:T(8,128)(2,1)S(1)}) custom-call(s32[1]{0:T(128)} %bitcast.1.lat_ref, s32[1]{0:T(128)} %bitcast.lon_ref, s32[48]{0:T(128)} %keep_hbm.1, s32[2,2,13]{2,1,0:T(2,128)} %lists_hbm.1, bf16[2,64,2048]{2,1,0:T(8,128)(2,1)} %q_hbm.1), custom_call_target="tpu_custom_call" | custom-call | bytes 1048576 | tf_op jit(solution)/shard_map/prepare/pallas_call | solution.py:315
  8.1 4.6 %collective-permute-start.3 = (bf16[17,64,128]{2,1,0:T(8,128)(2,1)S(1)}, bf16[17,64,128]{2,1,0:T(8,128)(2,1)S(1)}, u32[]{:S(2)}, u32[]{:S(2)}) collective-permute-start(bf16[17,64,128]{2,1,0:T(8,128)(2,1)S(1)} %get-tuple-element.10.after_ref.q0_ref), channel_id=1, source_target_pairs={{0,31},{1,2},{2,1},{3,4},{4,3},{5,6},{6,5},{7,8},{8,7},{9,10},{10,... | collective-permute-start | bytes 835592 | tf_op jit(solution)/shard_map/ppermute | solution.py:328
  12.7 2.2 %collective-permute-start.2 = (bf16[17,64,128]{2,1,0:T(8,128)(2,1)S(1)}, bf16[17,64,128]{2,1,0:T(8,128)(2,1)S(1)}, u32[]{:S(2)}, u32[]{:S(2)}) collective-permute-start(bf16[17,64,128]{2,1,0:T(8,128)(2,1)S(1)} %get-tuple-element.11.q1_ref), channel_id=1, source_target_pairs={{0,1},{1,0},{2,3},{3,2},{4,5},{5,4},{6,7},{7,6},{8,9},{9,8},{10,11... | collective-permute-start | bytes 835592 | tf_op jit(solution)/shard_map/ppermute | solution.py:328
  14.9 0.0 copy-start
  15.0 1.2 %copy-done = bf16[2,2,64,2048]{3,2,1,0:T(8,128)(2,1)S(1)} copy-done((bf16[2,2,64,2048]{3,2,1,0:T(8,128)(2,1)S(1)}, bf16[2,2,64,2048]{3,2,1,0:T(8,128)(2,1)}, u32[]{:S(2)}) %copy-start) | copy-done | bytes 1048600
  16.2 0.1 hold.1.own_ref
  16.2 4.5 %collective-permute-done.3.q_ref = bf16[17,64,128]{2,1,0:T(8,128)(2,1)S(1)} collective-permute-done((bf16[17,64,128]{2,1,0:T(8,128)(2,1)S(1)}, bf16[17,64,128]{2,1,0:T(8,128)(2,1)S(1)}, u32[]{:S(2)}, u32[]{:S(2)}) %collective-permute-start.3) | collective-permute-done | bytes 278560 | tf_op jit(solution)/shard_map/ppermute | solution.py:328
  20.7 0.0 collective-permute-done.far_ref
  20.7 0.0 collective-permute-done.1.near_ref
  20.7 1.0 %remote0.1 = bf16[17,64,128]{2,1,0:T(8,128)(2,1)S(1)} custom-call(s32[1]{0:T(128)} %bitcast.1.lat_ref, s32[1]{0:T(128)} %bitcast.lon_ref, bf16[17,64,128]{2,1,0:T(8,128)(2,1)S(1)} %collective-permute-done.3.q_ref, bf16[2,2,64,2048]{3,2,1,0:T(8,128)(2,1)S(1)} %collective-permute-done.far_ref, bf16[2,2,64,2048]{3,2,1,0:T(8,128)(2,1)S(1)} %hold.1.own_ref, ...), custom_call_target="tpu_custom_call" | custom-call | flops 268435456 | bytes 4194304 | tf_op jit(solution)/shard_map/remote0/pallas_call | solution.py:331
  21.8 4.5 %collective-permute-start.4 = (bf16[17,64,128]{2,1,0:T(8,128)(2,1)S(1)}, bf16[17,64,128]{2,1,0:T(8,128)(2,1)S(1)}, u32[]{:S(2)}, u32[]{:S(2)}) collective-permute-start(bf16[17,64,128]{2,1,0:T(8,128)(2,1)S(1)} %remote0.1), channel_id=1, source_target_pairs={{0,31},{1,2},{2,1},{3,4},{4,3},{5,6},{6,5},{7,8},{8,7},{9,10},{10,... | collective-permute-start | bytes 835592 | tf_op jit(solution)/shard_map/ppermute | solution.py:341
  26.3 0.0 collective-permute-done.2.q_ref
  26.3 1.1 %remote1.1.after_ref = bf16[17,64,128]{2,1,0:T(8,128)(2,1)S(1)} custom-call(s32[1]{0:T(128)} %bitcast.1.lat_ref, s32[1]{0:T(128)} %bitcast.lon_ref, bf16[17,64,128]{2,1,0:T(8,128)(2,1)S(1)} %collective-permute-done.2.q_ref, bf16[2,2,64,2048]{3,2,1,0:T(8,128)(2,1)S(1)} %collective-permute-done.far_ref, bf16[2,2,64,2048]{3,2,1,0:T(8,128)(2,1)S(1)} %hold.1.own_ref, ...), custom_call_target="tpu_custom_call" | custom-call | flops 268435456 | bytes 4194304 | tf_op jit(solution)/shard_map/remote1/pallas_call | solution.py:331
  27.4 1.9 %collective-permute-start.5 = (bf16[17,64,128]{2,1,0:T(8,128)(2,1)S(1)}, bf16[17,64,128]{2,1,0:T(8,128)(2,1)S(1)}, u32[]{:S(2)}, u32[]{:S(2)}) collective-permute-start(bf16[17,64,128]{2,1,0:T(8,128)(2,1)S(1)} %remote1.1.after_ref), channel_id=1, source_target_pairs={{0,1},{1,0},{2,3},{3,2},{4,5},{5,4},{6,7},{7,6},{8,9},{9,8},{10,11... | collective-permute-start | bytes 835592 | tf_op jit(solution)/shard_map/ppermute | solution.py:341
  29.3 2.0 %own.1 = (bf16[16,128,128]{2,1,0:T(8,128)(2,1)S(1)}, f32[128,128]{1,0:T(8,128)S(1)}, f32[128,128]{1,0:T(8,128)S(1)}) custom-call(s32[1]{0:T(128)} %bitcast.1.lat_ref, s32[1]{0:T(128)} %bitcast.lon_ref, bf16[17,64,128]{2,1,0:T(8,128)(2,1)S(1)} %get-tuple-element.10.after_ref.q0_ref, bf16[17,64,128]{2,1,0:T(8,128)(2,1)S(1)} %get-tuple-element.11.q1_ref, ...), custom_call_target="tpu_custom_call" | custom-call | flops 536870912 | bytes 4194304 | tf_op jit(solution)/shard_map/own/pallas_call | solution.py:342
  31.3 2.2 %collective-permute-done.4.part_ref = bf16[17,64,128]{2,1,0:T(8,128)(2,1)S(1)} collective-permute-done((bf16[17,64,128]{2,1,0:T(8,128)(2,1)S(1)}, bf16[17,64,128]{2,1,0:T(8,128)(2,1)S(1)}, u32[]{:S(2)}, u32[]{:S(2)}) %collective-permute-start.4) | collective-permute-done | bytes 278560 | tf_op jit(solution)/shard_map/ppermute | solution.py:341
  33.5 0.3 merge.1.first_ref
  33.8 2.9 %collective-permute-done.5.part_ref = bf16[17,64,128]{2,1,0:T(8,128)(2,1)S(1)} collective-permute-done((bf16[17,64,128]{2,1,0:T(8,128)(2,1)S(1)}, bf16[17,64,128]{2,1,0:T(8,128)(2,1)S(1)}, u32[]{:S(2)}, u32[]{:S(2)}) %collective-permute-start.5) | collective-permute-done | bytes 278560 | tf_op jit(solution)/shard_map/ppermute | solution.py:341
  36.7 1.2 %combine.1 = (bf16[2,64,2048]{2,1,0:T(8,128)(2,1)}, bf16[32,32,128]{2,1,0:T(8,128)(2,1)S(1)}, bf16[8,128]{1,0:T(8,128)(2,1)S(1)}) custom-call(s32[1]{0:T(128)} %bitcast.lon_ref, bf16[16,128,128]{2,1,0:T(8,128)(2,1)S(1)} %get-tuple-element.12.own_ref, f32[128,128]{1,0:T(8,128)S(1)} %get-tuple-element.13.top_ref, f32[128,128]{1,0:T(8,128)S(1)} %get-tuple-element.14.total_ref, ...), custom_call_target="tpu_custom_call" | custom-call | tf_op jit(solution)/shard_map/combine/pallas_call | solution.py:353
  37.9 22.9 %all_to_all.10.x_ref = bf16[32,32,128]{2,1,0:T(8,128)(2,1)S(1)} all-to-all(bf16[32,32,128]{2,1,0:T(8,128)(2,1)S(1)} %get-tuple-element.16), channel_id=1, replica_groups=mesh['lat'=24,'lon'=32] {'lon'}, dimensions={0} | all-to-all | bytes 524288 | tf_op jit(solution)/shard_map/all_to_all | solution.py:361
  60.8 0.1 total.1
  60.8 15.6 %all_to_all.11.x_ref = bf16[32,40,128]{2,1,0:T(8,128)(2,1)S(1)} all-to-all(bf16[32,40,128]{2,1,0:T(8,128)(2,1)S(1)} %total.1), channel_id=1, replica_groups=mesh['lat'=24,'lon'=32] {'lon'}, dimensions={0} | all-to-all | bytes 655360 | tf_op jit(solution)/shard_map/all_to_all | solution.py:363
  76.5 1.3 %unpack.1 = f32[1,16,128,128]{3,2,1,0:T(8,128)} custom-call(bf16[32,40,128]{2,1,0:T(8,128)(2,1)S(1)} %all_to_all.11.x_ref), custom_call_target="tpu_custom_call" | custom-call | tf_op jit(solution)/shard_map/unpack/pallas_call | solution.py:365
Async XLA Ops:
  0.6 20.1 %collective-permute-start = (bf16[2,2,64,2048]{3,2,1,0:T(8,128)(2,1)}, bf16[2,2,64,2048]{3,2,1,0:T(8,128)(2,1)S(1)}, u32[]{:S(2)}, u32[]{:S(2)}) collective-permute-start(bf16[2,2,64,2048]{3,2,1,0:T(8,128)(2,1)} %x_ref.1), channel_id=1, source_target_pairs={{32,64},{64,32},{96,128},{128,96},{160,192},{192,160},{224,256},{2... | collective-permute-start | bytes 3145736 | tf_op jit(solution)/shard_map/ppermute | solution.py:311
  1.4 19.4 %collective-permute-start.1 = (bf16[2,2,64,2048]{3,2,1,0:T(8,128)(2,1)}, bf16[2,2,64,2048]{3,2,1,0:T(8,128)(2,1)S(1)}, u32[]{:S(2)}, u32[]{:S(2)}) collective-permute-start(bf16[2,2,64,2048]{3,2,1,0:T(8,128)(2,1)} %x_ref.1), channel_id=1, source_target_pairs={{0,32},{32,0},{64,96},{96,64},{128,160},{160,128},{192,224},{224,1... | collective-permute-start | bytes 3145736 | tf_op jit(solution)/shard_map/ppermute | solution.py:312
  8.1 12.6 %collective-permute-start.3 = (bf16[17,64,128]{2,1,0:T(8,128)(2,1)S(1)}, bf16[17,64,128]{2,1,0:T(8,128)(2,1)S(1)}, u32[]{:S(2)}, u32[]{:S(2)}) collective-permute-start(bf16[17,64,128]{2,1,0:T(8,128)(2,1)S(1)} %get-tuple-element.10.after_ref.q0_ref), channel_id=1, source_target_pairs={{0,31},{1,2},{2,1},{3,4},{4,3},{5,6},{6,5},{7,8},{8,7},{9,10},{10,... | collective-permute-start | bytes 835592 | tf_op jit(solution)/shard_map/ppermute | solution.py:328
  12.7 13.6 %collective-permute-start.2 = (bf16[17,64,128]{2,1,0:T(8,128)(2,1)S(1)}, bf16[17,64,128]{2,1,0:T(8,128)(2,1)S(1)}, u32[]{:S(2)}, u32[]{:S(2)}) collective-permute-start(bf16[17,64,128]{2,1,0:T(8,128)(2,1)S(1)} %get-tuple-element.11.q1_ref), channel_id=1, source_target_pairs={{0,1},{1,0},{2,3},{3,2},{4,5},{5,4},{6,7},{7,6},{8,9},{9,8},{10,11... | collective-permute-start | bytes 835592 | tf_op jit(solution)/shard_map/ppermute | solution.py:328
  14.9 1.2 %copy-start = (bf16[2,2,64,2048]{3,2,1,0:T(8,128)(2,1)S(1)}, bf16[2,2,64,2048]{3,2,1,0:T(8,128)(2,1)}, u32[]{:S(2)}) copy-start(bf16[2,2,64,2048]{3,2,1,0:T(8,128)(2,1)} %x_ref.1) | copy-start | bytes 3145732
  21.8 11.7 %collective-permute-start.4 = (bf16[17,64,128]{2,1,0:T(8,128)(2,1)S(1)}, bf16[17,64,128]{2,1,0:T(8,128)(2,1)S(1)}, u32[]{:S(2)}, u32[]{:S(2)}) collective-permute-start(bf16[17,64,128]{2,1,0:T(8,128)(2,1)S(1)} %remote0.1), channel_id=1, source_target_pairs={{0,31},{1,2},{2,1},{3,4},{4,3},{5,6},{6,5},{7,8},{8,7},{9,10},{10,... | collective-permute-start | bytes 835592 | tf_op jit(solution)/shard_map/ppermute | solution.py:341
  27.4 9.3 %collective-permute-start.5 = (bf16[17,64,128]{2,1,0:T(8,128)(2,1)S(1)}, bf16[17,64,128]{2,1,0:T(8,128)(2,1)S(1)}, u32[]{:S(2)}, u32[]{:S(2)}) collective-permute-start(bf16[17,64,128]{2,1,0:T(8,128)(2,1)S(1)} %remote1.1.after_ref), channel_id=1, source_target_pairs={{0,1},{1,0},{2,3},{3,2},{4,5},{5,4},{6,7},{7,6},{8,9},{9,8},{10,11... | collective-permute-start | bytes 835592 | tf_op jit(solution)/shard_map/ppermute | solution.py:341

commit v5 on v4

--- a/solution.py
+++ b/solution.py
@@ -36,12 +36,15 @@
 def prepare_body(rows_total, lat_ref, lon_ref, keep_hbm, lists_hbm, q_hbm, out0_ref, out1_ref, keep_ref, lists_ref, q_ref, sems):
     copies = [
         pltpu.make_async_copy(src, dst, sems.at[i])
-        for i, (src, dst) in enumerate(((lists_hbm, lists_ref), (keep_hbm, keep_ref), (q_hbm, q_ref)))
+        for i, (src, dst) in enumerate(((lists_hbm, lists_ref), (keep_hbm, keep_ref)))
     ]
+    first = lat_ref[0] * 2
+    _, odd = place(lat_ref, lon_ref)
+    for i, b in enumerate((odd, 1 - odd)):
+        cells = pl.ds(pl.multiple_of(b * BLOCK, BLOCK), BLOCK)
+        copies.append(pltpu.make_async_copy(q_hbm.at[:, cells, :], q_ref.at[:, cells, :], sems.at[2 + i]))
     for copy in copies:
         copy.start()
-    first = lat_ref[0] * 2
-    _, odd = place(lat_ref, lon_ref)
     lane = iota((1, 128), 1)
     copies[0].wait()
     copies[1].wait()
@@ -62,8 +65,8 @@
             seen = jnp.where((listed == 1) & (usable == 1), 1.0, 0.0)
             seen = jnp.broadcast_to(seen, (BLOCK, 128)).astype(jnp.bfloat16)
             out[HEADS, t * BLOCK : (t + 1) * BLOCK, :] = seen
-    copies[2].wait()
-    for b, out in ((odd, out0_ref), (1 - odd, out1_ref)):
+    for b, out, copy in ((odd, out0_ref, copies[2]), (1 - odd, out1_ref, copies[3])):
+        copy.wait()
         cells = pl.ds(pl.multiple_of(b * BLOCK, BLOCK), BLOCK)
         for t in range(2):
             for h in range(HEADS):
@@ -322,7 +325,7 @@
             pltpu.SMEM(keep.shape, jnp.int32),
             pltpu.SMEM(lists.shape, jnp.int32),
             pltpu.VMEM(queries.shape, bf16),
-            pltpu.SemaphoreType.DMA((3,)),
+            pltpu.SemaphoreType.DMA((4,)),
         ],
     )(lat, lon, *[pltpu.with_memory_space_constraint(x, pltpu.HBM) for x in (keep, lists, queries)])
     theirs = [lax.ppermute(x, "lon", pair) for x, pair in zip(mine, pairs)]

time: 78.1 us -> 78.1 us (level)
  no operation moved by 1% of the time
where the time goes in v5:
time: 78.1 us; the launch traced here: 77.7 us
  blocking collectives  38.5 us (49%)
  starting transfers between devices  19.6 us (25%)
  waiting for transfers between devices  9.59 us (12%)
  Pallas kernels  8.06 us (10%)
  local copies, waits for them, and re-layouts  1.22 us (2%)
    all_to_all x1, blocking collectives, local(): swapped = lax.all_to_all(packed, 'lon', 0, 0, tiled=True)  22.9 us
    all_to_all x1, blocking collectives, local(): gathered = lax.all_to_all(summed, 'lon', 0, 0, tiled=True)  15.6 us
    ppermute x2, starting transfers between devices, local(): theirs = [lax.ppermute(x, 'lon', pair) for x, pair in zip(mine, pairs)]  6.8 us
    ppermute x2, starting transfers between devices, local(): parts = [lax.ppermute(x, 'lon', pair) for x, pair in zip(answers, pairs)]  6.46 us
    ppermute x1, starting transfers between devices, local(): near = lax.ppermute(keyval, 'lat', cores)  5.58 us
    ppermute x2, waiting for transfers between devices, local(): parts = [lax.ppermute(x, 'lon', pair) for x, pair in zip(answers, pairs)]  5.12 us
    ppermute x2, waiting for transfers between devices, local(): theirs = [lax.ppermute(x, 'lon', pair) for x, pair in zip(mine, pairs)]  4.47 us
    pallas_call x2, Pallas kernels, local(): call(functools.partial(remote_body, i), [edge], [SMEM, SMEM] + [VMEM] * 4...  2.1 us
  transfers between devices with their start and end apart: 6, of which 3 were waited for; matrix products, arithmetic and copies ran while one was open for 0% of the time, Pallas kernels for 7%

profile of v5, /device:TPU:8, one launch (start us, length us, event | category | flops | bytes accessed | tf_op | source)
XLA Modules:
  0.0 77.7 jit_solution(3500786732643341661)
XLA Ops:
  0.6 0.7 collective-permute-start
  1.4 5.6 %collective-permute-start.1 = (bf16[2,2,64,2048]{3,2,1,0:T(8,128)(2,1)}, bf16[2,2,64,2048]{3,2,1,0:T(8,128)(2,1)S(1)}, u32[]{:S(2)}, u32[]{:S(2)}) collective-permute-start(bf16[2,2,64,2048]{3,2,1,0:T(8,128)(2,1)} %x_ref.1), channel_id=1, source_target_pairs={{0,32},{32,0},{64,96},{96,64},{128,160},{160,128},{192,224},{224,1... | collective-permute-start | bytes 3145736 | tf_op jit(solution)/shard_map/ppermute | solution.py:315
  7.0 1.1 %prepare.1 = (bf16[17,64,128]{2,1,0:T(8,128)(2,1)S(1)}, bf16[17,64,128]{2,1,0:T(8,128)(2,1)S(1)}) custom-call(s32[1]{0:T(128)} %bitcast.1.lat_ref, s32[1]{0:T(128)} %bitcast.lon_ref, s32[48]{0:T(128)} %keep_hbm.1, s32[2,2,13]{2,1,0:T(2,128)} %lists_hbm.1, bf16[2,64,2048]{2,1,0:T(8,128)(2,1)} %q_hbm.1), custom_call_target="tpu_custom_call" | custom-call | bytes 1048576 | tf_op jit(solution)/shard_map/prepare/pallas_call | solution.py:318
  8.1 4.6 %collective-permute-start.3 = (bf16[17,64,128]{2,1,0:T(8,128)(2,1)S(1)}, bf16[17,64,128]{2,1,0:T(8,128)(2,1)S(1)}, u32[]{:S(2)}, u32[]{:S(2)}) collective-permute-start(bf16[17,64,128]{2,1,0:T(8,128)(2,1)S(1)} %get-tuple-element.10.after_ref.q0_ref), channel_id=1, source_target_pairs={{0,31},{1,2},{2,1},{3,4},{4,3},{5,6},{6,5},{7,8},{8,7},{9,10},{10,... | collective-permute-start | bytes 835592 | tf_op jit(solution)/shard_map/ppermute | solution.py:331
  12.6 2.2 %collective-permute-start.2 = (bf16[17,64,128]{2,1,0:T(8,128)(2,1)S(1)}, bf16[17,64,128]{2,1,0:T(8,128)(2,1)S(1)}, u32[]{:S(2)}, u32[]{:S(2)}) collective-permute-start(bf16[17,64,128]{2,1,0:T(8,128)(2,1)S(1)} %get-tuple-element.11.q1_ref), channel_id=1, source_target_pairs={{0,1},{1,0},{2,3},{3,2},{4,5},{5,4},{6,7},{7,6},{8,9},{9,8},{10,11... | collective-permute-start | bytes 835592 | tf_op jit(solution)/shard_map/ppermute | solution.py:331
  14.9 0.0 copy-start
  14.9 1.2 %copy-done = bf16[2,2,64,2048]{3,2,1,0:T(8,128)(2,1)S(1)} copy-done((bf16[2,2,64,2048]{3,2,1,0:T(8,128)(2,1)S(1)}, bf16[2,2,64,2048]{3,2,1,0:T(8,128)(2,1)}, u32[]{:S(2)}) %copy-start) | copy-done | bytes 1048600
  16.1 0.1 hold.1.own_ref
  16.2 4.5 %collective-permute-done.3.q_ref = bf16[17,64,128]{2,1,0:T(8,128)(2,1)S(1)} collective-permute-done((bf16[17,64,128]{2,1,0:T(8,128)(2,1)S(1)}, bf16[17,64,128]{2,1,0:T(8,128)(2,1)S(1)}, u32[]{:S(2)}, u32[]{:S(2)}) %collective-permute-start.3) | collective-permute-done | bytes 278560 | tf_op jit(solution)/shard_map/ppermute | solution.py:331
  20.7 0.0 collective-permute-done.far_ref
  20.7 0.0 collective-permute-done.1.near_ref
  20.7 1.0 %remote0.1 = bf16[17,64,128]{2,1,0:T(8,128)(2,1)S(1)} custom-call(s32[1]{0:T(128)} %bitcast.1.lat_ref, s32[1]{0:T(128)} %bitcast.lon_ref, bf16[17,64,128]{2,1,0:T(8,128)(2,1)S(1)} %collective-permute-done.3.q_ref, bf16[2,2,64,2048]{3,2,1,0:T(8,128)(2,1)S(1)} %collective-permute-done.far_ref, bf16[2,2,64,2048]{3,2,1,0:T(8,128)(2,1)S(1)} %hold.1.own_ref, ...), custom_call_target="tpu_custom_call" | custom-call | flops 268435456 | bytes 4194304 | tf_op jit(solution)/shard_map/remote0/pallas_call | solution.py:334
  21.7 4.5 %collective-permute-start.4 = (bf16[17,64,128]{2,1,0:T(8,128)(2,1)S(1)}, bf16[17,64,128]{2,1,0:T(8,128)(2,1)S(1)}, u32[]{:S(2)}, u32[]{:S(2)}) collective-permute-start(bf16[17,64,128]{2,1,0:T(8,128)(2,1)S(1)} %remote0.1), channel_id=1, source_target_pairs={{0,31},{1,2},{2,1},{3,4},{4,3},{5,6},{6,5},{7,8},{8,7},{9,10},{10,... | collective-permute-start | bytes 835592 | tf_op jit(solution)/shard_map/ppermute | solution.py:344
  26.3 0.0 collective-permute-done.2.q_ref
  26.3 1.1 %remote1.1.after_ref = bf16[17,64,128]{2,1,0:T(8,128)(2,1)S(1)} custom-call(s32[1]{0:T(128)} %bitcast.1.lat_ref, s32[1]{0:T(128)} %bitcast.lon_ref, bf16[17,64,128]{2,1,0:T(8,128)(2,1)S(1)} %collective-permute-done.2.q_ref, bf16[2,2,64,2048]{3,2,1,0:T(8,128)(2,1)S(1)} %collective-permute-done.far_ref, bf16[2,2,64,2048]{3,2,1,0:T(8,128)(2,1)S(1)} %hold.1.own_ref, ...), custom_call_target="tpu_custom_call" | custom-call | flops 268435456 | bytes 4194304 | tf_op jit(solution)/shard_map/remote1/pallas_call | solution.py:334
  27.3 1.9 %collective-permute-start.5 = (bf16[17,64,128]{2,1,0:T(8,128)(2,1)S(1)}, bf16[17,64,128]{2,1,0:T(8,128)(2,1)S(1)}, u32[]{:S(2)}, u32[]{:S(2)}) collective-permute-start(bf16[17,64,128]{2,1,0:T(8,128)(2,1)S(1)} %remote1.1.after_ref), channel_id=1, source_target_pairs={{0,1},{1,0},{2,3},{3,2},{4,5},{5,4},{6,7},{7,6},{8,9},{9,8},{10,11... | collective-permute-start | bytes 835592 | tf_op jit(solution)/shard_map/ppermute | solution.py:344
  29.3 2.0 %own.1 = (bf16[16,128,128]{2,1,0:T(8,128)(2,1)S(1)}, f32[128,128]{1,0:T(8,128)S(1)}, f32[128,128]{1,0:T(8,128)S(1)}) custom-call(s32[1]{0:T(128)} %bitcast.1.lat_ref, s32[1]{0:T(128)} %bitcast.lon_ref, bf16[17,64,128]{2,1,0:T(8,128)(2,1)S(1)} %get-tuple-element.10.after_ref.q0_ref, bf16[17,64,128]{2,1,0:T(8,128)(2,1)S(1)} %get-tuple-element.11.q1_ref, ...), custom_call_target="tpu_custom_call" | custom-call | flops 536870912 | bytes 4194304 | tf_op jit(solution)/shard_map/own/pallas_call | solution.py:345
  31.2 2.2 %collective-permute-done.4.part_ref = bf16[17,64,128]{2,1,0:T(8,128)(2,1)S(1)} collective-permute-done((bf16[17,64,128]{2,1,0:T(8,128)(2,1)S(1)}, bf16[17,64,128]{2,1,0:T(8,128)(2,1)S(1)}, u32[]{:S(2)}, u32[]{:S(2)}) %collective-permute-start.4) | collective-permute-done | bytes 278560 | tf_op jit(solution)/shard_map/ppermute | solution.py:344
  33.4 0.3 merge.1.first_ref
  33.8 2.9 %collective-permute-done.5.part_ref = bf16[17,64,128]{2,1,0:T(8,128)(2,1)S(1)} collective-permute-done((bf16[17,64,128]{2,1,0:T(8,128)(2,1)S(1)}, bf16[17,64,128]{2,1,0:T(8,128)(2,1)S(1)}, u32[]{:S(2)}, u32[]{:S(2)}) %collective-permute-start.5) | collective-permute-done | bytes 278560 | tf_op jit(solution)/shard_map/ppermute | solution.py:344
  36.7 1.2 %combine.1 = (bf16[2,64,2048]{2,1,0:T(8,128)(2,1)}, bf16[32,32,128]{2,1,0:T(8,128)(2,1)S(1)}, bf16[8,128]{1,0:T(8,128)(2,1)S(1)}) custom-call(s32[1]{0:T(128)} %bitcast.lon_ref, bf16[16,128,128]{2,1,0:T(8,128)(2,1)S(1)} %get-tuple-element.12.own_ref, f32[128,128]{1,0:T(8,128)S(1)} %get-tuple-element.13.top_ref, f32[128,128]{1,0:T(8,128)S(1)} %get-tuple-element.14.total_ref, ...), custom_call_target="tpu_custom_call" | custom-call | tf_op jit(solution)/shard_map/combine/pallas_call | solution.py:356
  37.8 22.9 %all_to_all.10.x_ref = bf16[32,32,128]{2,1,0:T(8,128)(2,1)S(1)} all-to-all(bf16[32,32,128]{2,1,0:T(8,128)(2,1)S(1)} %get-tuple-element.16), channel_id=1, replica_groups=mesh['lat'=24,'lon'=32] {'lon'}, dimensions={0} | all-to-all | bytes 524288 | tf_op jit(solution)/shard_map/all_to_all | solution.py:364
  60.7 0.1 total.1
  60.8 15.6 %all_to_all.11.x_ref = bf16[32,40,128]{2,1,0:T(8,128)(2,1)S(1)} all-to-all(bf16[32,40,128]{2,1,0:T(8,128)(2,1)S(1)} %total.1), channel_id=1, replica_groups=mesh['lat'=24,'lon'=32] {'lon'}, dimensions={0} | all-to-all | bytes 655360 | tf_op jit(solution)/shard_map/all_to_all | solution.py:366
  76.4 1.3 %unpack.1 = f32[1,16,128,128]{3,2,1,0:T(8,128)} custom-call(bf16[32,40,128]{2,1,0:T(8,128)(2,1)S(1)} %all_to_all.11.x_ref), custom_call_target="tpu_custom_call" | custom-call | tf_op jit(solution)/shard_map/unpack/pallas_call | solution.py:368
Async XLA Ops:
  0.6 20.0 %collective-permute-start = (bf16[2,2,64,2048]{3,2,1,0:T(8,128)(2,1)}, bf16[2,2,64,2048]{3,2,1,0:T(8,128)(2,1)S(1)}, u32[]{:S(2)}, u32[]{:S(2)}) collective-permute-start(bf16[2,2,64,2048]{3,2,1,0:T(8,128)(2,1)} %x_ref.1), channel_id=1, source_target_pairs={{32,64},{64,32},{96,128},{128,96},{160,192},{192,160},{224,256},{2... | collective-permute-start | bytes 3145736 | tf_op jit(solution)/shard_map/ppermute | solution.py:314
  1.4 19.3 %collective-permute-start.1 = (bf16[2,2,64,2048]{3,2,1,0:T(8,128)(2,1)}, bf16[2,2,64,2048]{3,2,1,0:T(8,128)(2,1)S(1)}, u32[]{:S(2)}, u32[]{:S(2)}) collective-permute-start(bf16[2,2,64,2048]{3,2,1,0:T(8,128)(2,1)} %x_ref.1), channel_id=1, source_target_pairs={{0,32},{32,0},{64,96},{96,64},{128,160},{160,128},{192,224},{224,1... | collective-permute-start | bytes 3145736 | tf_op jit(solution)/shard_map/ppermute | solution.py:315
  8.1 12.6 %collective-permute-start.3 = (bf16[17,64,128]{2,1,0:T(8,128)(2,1)S(1)}, bf16[17,64,128]{2,1,0:T(8,128)(2,1)S(1)}, u32[]{:S(2)}, u32[]{:S(2)}) collective-permute-start(bf16[17,64,128]{2,1,0:T(8,128)(2,1)S(1)} %get-tuple-element.10.after_ref.q0_ref), channel_id=1, source_target_pairs={{0,31},{1,2},{2,1},{3,4},{4,3},{5,6},{6,5},{7,8},{8,7},{9,10},{10,... | collective-permute-start | bytes 835592 | tf_op jit(solution)/shard_map/ppermute | solution.py:331
  12.6 13.6 %collective-permute-start.2 = (bf16[17,64,128]{2,1,0:T(8,128)(2,1)S(1)}, bf16[17,64,128]{2,1,0:T(8,128)(2,1)S(1)}, u32[]{:S(2)}, u32[]{:S(2)}) collective-permute-start(bf16[17,64,128]{2,1,0:T(8,128)(2,1)S(1)} %get-tuple-element.11.q1_ref), channel_id=1, source_target_pairs={{0,1},{1,0},{2,3},{3,2},{4,5},{5,4},{6,7},{7,6},{8,9},{9,8},{10,11... | collective-permute-start | bytes 835592 | tf_op jit(solution)/shard_map/ppermute | solution.py:331
  14.9 1.2 %copy-start = (bf16[2,2,64,2048]{3,2,1,0:T(8,128)(2,1)S(1)}, bf16[2,2,64,2048]{3,2,1,0:T(8,128)(2,1)}, u32[]{:S(2)}) copy-start(bf16[2,2,64,2048]{3,2,1,0:T(8,128)(2,1)} %x_ref.1) | copy-start | bytes 3145732
  21.7 11.7 %collective-permute-start.4 = (bf16[17,64,128]{2,1,0:T(8,128)(2,1)S(1)}, bf16[17,64,128]{2,1,0:T(8,128)(2,1)S(1)}, u32[]{:S(2)}, u32[]{:S(2)}) collective-permute-start(bf16[17,64,128]{2,1,0:T(8,128)(2,1)S(1)} %remote0.1), channel_id=1, source_target_pairs={{0,31},{1,2},{2,1},{3,4},{4,3},{5,6},{6,5},{7,8},{8,7},{9,10},{10,... | collective-permute-start | bytes 835592 | tf_op jit(solution)/shard_map/ppermute | solution.py:344
  27.3 9.3 %collective-permute-start.5 = (bf16[17,64,128]{2,1,0:T(8,128)(2,1)S(1)}, bf16[17,64,128]{2,1,0:T(8,128)(2,1)S(1)}, u32[]{:S(2)}, u32[]{:S(2)}) collective-permute-start(bf16[17,64,128]{2,1,0:T(8,128)(2,1)S(1)} %remote1.1.after_ref), channel_id=1, source_target_pairs={{0,1},{1,0},{2,3},{3,2},{4,5},{5,4},{6,7},{7,6},{8,9},{9,8},{10,11... | collective-permute-start | bytes 835592 | tf_op jit(solution)/shard_map/ppermute | solution.py:344
